TPU v7x, 512 devices: a whole 4x8x8 slice. The times are simulated.
512 devices in a mesh: row: 32 (over x_lo, y, core), col: 16 (over x_hi, z).
Axes of the slice: x: 4 (x_hi: 2, x_lo: 2; x = x_hi * 2 + x_lo), y: 8, z: 8, core: 2. Of those that a mesh axis runs over, the one named last changes fastest.
Arguments:
- front_init: float32 [16, 16, 2, 4096], P(None, None, None, 'row'), may hold values from -3 to 3
- green_hist: float32 [256, 16, 2, 4096], P('row', None, None, 'col'), may hold values from -0.0625 to 0.0625
- field_hist: float32 [256, 16, 2, 4096], P('row', None, None, 'col'), may hold values from -0.0625 to 0.0625
Outputs:
- front_final: float32 [16, 16, 2, 4096], P(None, None, None, 'row')
All inputs are finite; a program needn't handle non-finite values.
Results may differ from a plain program's by a relative error of at most 0.0001.
Values sent between devices are 32-bit elements; how exact they have to be, the bound alone decides.
No kernel may reach another device: no remote copies, remote signals or barrier semaphores. Data moves between devices by JAX's collectives and lax.ppermute only.
A program may use at most 64 MiB of HBM per device.

v0:
```python
import functools

import jax
import jax.numpy as jnp
from jax import lax
from jax.experimental import pallas as pl
from jax.experimental.pallas import tpu as pltpu
from jax.sharding import Mesh, PartitionSpec as P


STEP_WEIGHT = 0.5

A = ("xl", "y")
B = ("xh", "z")
EVERY = ("xl", "y", "core", "xh", "z")


def split(value):
    high = value.astype(jnp.bfloat16)
    low = (value - high.astype(jnp.float32)).astype(jnp.bfloat16)
    return high, low


def dot3(left, right):
    def one(x, y):
        return jnp.dot(x, y, preferred_element_type=jnp.float32)

    return one(left[0], right[0]) + (one(left[0], right[1]) + one(left[1], right[0]))


def swap_orbitals(value, orbits):
    rows, lanes = value.shape
    row = lax.broadcasted_iota(jnp.int32, value.shape, 0)
    lane = lax.broadcasted_iota(jnp.int32, value.shape, 1)
    step = 1
    while step < orbits:
        row_bit = (row // step) % 2
        lane_bit = (lane // step) % 2
        up = pltpu.roll(pltpu.roll(value, step, 1), rows - step, 0)
        down = pltpu.roll(pltpu.roll(value, lanes - step, 1), step, 0)
        value = jnp.where(row_bit == lane_bit, value, jnp.where(row_bit == 0, up, down))
        step *= 2
    return value


def sigma_pair(re, im, orbits):
    other_re = swap_orbitals(re, orbits)
    other_im = swap_orbitals(im, orbits)
    square_re = re * re - im * im
    square_im = 2.0 * re * im
    return (
        square_re * other_re + square_im * other_im,
        square_im * other_re - square_re * other_im,
    )


def history(refs, part):
    depth = refs[0].shape[0] // 4
    halves = [
        jnp.concatenate([ref[pl.ds(2 * half + part, depth, stride=4), :] for ref in refs], axis=0)
        for half in range(2)
    ]
    return jnp.concatenate(halves, axis=1)


def image_of(left_re, left_im, refs):
    left_re, left_im = split(left_re), split(left_im)
    right_re, right_im = split(history(refs, 0)), split(history(refs, 1))
    return (
        dot3(left_re, right_re) - dot3(left_im, right_im),
        dot3(left_re, right_im) + dot3(left_im, right_re),
    )


def put(target_ref, part, image, orbits, order):
    lanes = target_ref.shape[1]
    for half in range(2):
        for place, front in enumerate(order):
            first = (half * len(order) + place) * 2 * orbits + part
            target_ref[pl.ds(first, orbits, stride=2), :] = image[
                front * orbits:(front + 1) * orbits, half * lanes:(half + 1) * lanes]


def first_kernel(orbits, order, init_ref, green_ref, field_ref,
                 own_ref, other_ref, near_ref, last_ref, init, green, field, sems):
    copies = [
        pltpu.make_async_copy(source, target, sems.at[n])
        for n, (source, target) in enumerate(
            ((init_ref, init), (green_ref, green), (field_ref, field)))
    ]
    for copy in copies:
        copy.start()
    core, xh, z = (lax.axis_index(axis) for axis in ("core", "xh", "z"))
    fronts = len(order)
    piece = 2 * orbits
    rows = init.shape[0]

    def front(index):
        return init[pl.ds(pl.multiple_of(index * piece, piece), piece), :]

    copies[0].wait()
    near_ref[...] = front(core * fronts + z)
    last_ref[...] = front(xh * fronts + z)
    other_ref[rows:, :] = front((1 - core) * fronts + z)
    re = init[pl.ds(0, rows // 2, stride=2), :]
    im = init[pl.ds(1, rows // 2, stride=2), :]
    sigma_re, sigma_im = sigma_pair(re, im, orbits)
    left_re = jnp.concatenate([sigma_re, re], axis=1)
    left_im = jnp.concatenate([sigma_im, im], axis=1)
    copies[1].wait()
    copies[2].wait()
    images = image_of(left_re, left_im, (green, field))
    cut = rows // 4
    for part, image in enumerate(images):
        low, high = image[:cut], image[cut:]
        put(own_ref, part, jnp.where(core == 0, low, high), orbits, order)
        put(other_ref, part, jnp.where(core == 0, high, low), orbits, order)


def second_kernel(orbits, order, front_ref, green_ref, field_ref, green_far, field_far, out_ref):
    core = lax.axis_index("core")
    half_rows = front_ref.shape[0] // 2

    def part_of(part):
        halves = [
            front_ref[pl.ds(half * half_rows + part, half_rows // 2, stride=2), :]
            for half in range(2)
        ]
        return jnp.where(core == 0, halves[0], halves[1]), jnp.where(core == 0, halves[1], halves[0])

    left_re, left_im = [], []
    for re, im in zip(part_of(0), part_of(1)):
        sigma_re, sigma_im = sigma_pair(re, im, orbits)
        left_re += [sigma_re, re]
        left_im += [sigma_im, im]
    images = image_of(
        jnp.concatenate(left_re, axis=1), jnp.concatenate(left_im, axis=1),
        (green_ref, field_ref, green_far, field_far))
    for part, image in enumerate(images):
        put(out_ref, part, image, orbits, order)


VMEM = pl.BlockSpec(memory_space=pltpu.VMEM)
LIMIT = pltpu.CompilerParams(vmem_limit_bytes=12 << 20)


def first_collide(init, green, field, orbits, order):
    rows, width = init.shape
    operands = [pltpu.with_memory_space_constraint(x, pltpu.HBM) for x in (init, green, field)]
    return pl.pallas_call(
        functools.partial(first_kernel, orbits, order),
        out_shape=[
            jax.ShapeDtypeStruct((n, width), jnp.float32)
            for n in (rows, rows + 2 * orbits, 2 * orbits, 2 * orbits)
        ],
        in_specs=[pl.BlockSpec(memory_space=pltpu.HBM)] * 3,
        out_specs=[VMEM] * 4,
        scratch_shapes=[pltpu.VMEM(x.shape, x.dtype) for x in (init, green, field)]
        + [pltpu.SemaphoreType.DMA((3,))],
        compiler_params=LIMIT,
        name="first_collide",
    )(*operands)


def second_collide(front, histories, orbits, order):
    return pl.pallas_call(
        functools.partial(second_kernel, orbits, order),
        out_shape=jax.ShapeDtypeStruct(front.shape, jnp.float32),
        in_specs=[VMEM] * 5,
        out_specs=VMEM,
        compiler_params=LIMIT,
        name="second_collide",
    )(front, *histories)


def per_device(turns, ys, zs, front_init, green_hist, field_hist):
    return corrector(turns, ys, zs, front_init, green_hist, field_hist)


def corrector(turns, ys, zs, front_init, green_hist, field_hist):
    fronts, orbits, parts, width = front_init.shape
    rows = fronts * orbits * parts
    init = front_init.reshape(rows, width)

    def tiles(history):
        times, inner, _, lanes = history.shape
        return history.reshape(times, inner, parts, lanes // width, width).transpose(
            0, 1, 3, 2, 4).reshape(-1, width)

    def swap(value):
        return lax.ppermute(value, "core", [(0, 1), (1, 0)])

    def reduced(partial_sum):
        spread = lax.all_to_all(partial_sum.reshape(fronts, -1, width), A, 0, 0, tiled=True)
        return jnp.sum(spread, axis=0)

    def gathered(copies):
        return lax.all_to_all(copies, B, 0, 0, tiled=True).reshape(rows, width)

    def copies_of(start, turned):
        piece = start + STEP_WEIGHT * turned
        return jnp.broadcast_to(piece[None], (fronts,) + piece.shape)

    green, field = tiles(green_hist), tiles(field_hist)
    order = [(y + zs // 2) % zs for y in range(ys)]
    own, other, near, last = first_collide(init, green, field, orbits, order)
    arrived = swap(other)
    piece = reduced(own + arrived[:rows])
    near = jnp.where(lax.axis_index("xh") == lax.axis_index("core"), near, arrived[rows:])
    green_late, field_late, piece = lax.optimization_barrier((green, field, piece))
    turned = lax.ppermute(piece, EVERY, turns[0])
    green_far = swap(green_late)
    field_far = swap(field_late)
    copies = copies_of(near, turned)
    green_far, field_far, copies = lax.optimization_barrier((green_far, field_far, copies))
    current = gathered(copies)
    image = second_collide(current, (green, field, green_far, field_far), orbits, order)
    turned = lax.ppermute(reduced(image), EVERY, turns[1])
    return gathered(copies_of(last, turned)).reshape(front_init.shape)


def solution(mesh):
    xls, ys, cores, xhs, zs = 2, 8, 2, 2, 8
    fine = Mesh(mesh.devices.reshape(xls, ys, cores, xhs, zs), EVERY)

    def place(xl, y, core, xh, z):
        return (((xl * ys + y) * cores + core) * xhs + xh) * zs + z

    everyone = [
        (xl, y, core, xh, z)
        for xl in range(xls) for y in range(ys) for core in range(cores)
        for xh in range(xhs) for z in range(zs)
    ]
    turns = [
        [(place(xl, y, core, xh, z), place(xh, z, core, xl, (y + zs // 2) % zs))
         for xl, y, core, xh, z in everyone],
        [(place(xl, y, core, xh, z), place(xh, z, xl, core, (y + zs // 2) % zs))
         for xl, y, core, xh, z in everyone],
    ]
    return jax.shard_map(
        functools.partial(per_device, turns, ys, zs),
        mesh=fine,
        in_specs=(
            P(None, None, None, ("xl", "y", "core")),
            P(("xl", "y", "core"), None, None, B),
            P(("xl", "y", "core"), None, None, B),
        ),
        out_specs=P(None, None, None, ("xl", "y", "core")),
        check_vma=False,
    )
```

profile of v0, /device:TPU:8, one launch (start us, length us, event | category | flops | bytes accessed | tf_op | source)
XLA Modules:
  0.0 105.1 jit_solution(8248532692384951373)
XLA Ops:
  0.0 2.5 %first_collide.1 = (f32[512,128]{1,0:T(8,128)S(1)}, f32[544,128]{1,0:T(8,128)S(1)}, f32[32,128]{1,0:T(8,128)S(1)}, f32[32,128]{1,0:T(8,128)S(1)}) custom-call(f32[512,128]{1,0:T(8,128)} %bitcast.25, f32[512,128]{1,0:T(8,128)} %bitcast.15, f32[512,128]{1,0:T(8,128)} %bitcast.18), custom_call_target="tpu_custom_call" | custom-call | tf_op jit(solution)/shard_map/first_collide/pallas_call | solution.py:150
  2.5 1.9 %collective-permute-start = (f32[544,128]{1,0:T(8,128)S(1)}, f32[544,128]{1,0:T(8,128)S(1)}, u32[]{:S(2)}, u32[]{:S(2)}) collective-permute-start(f32[544,128]{1,0:T(8,128)S(1)} %get-tuple-element.17), channel_id=1, source_target_pairs={{0,16},{16,0},{1,17},{17,1},{2,18},{18,2},{3,19},{19,3},{4,20},{20... | collective-permute-start | bytes 835592 | tf_op jit(solution)/shard_map/ppermute | solution.py:191
  4.4 1.5 %collective-permute-done = f32[544,128]{1,0:T(8,128)S(1)} collective-permute-done((f32[544,128]{1,0:T(8,128)S(1)}, f32[544,128]{1,0:T(8,128)S(1)}, u32[]{:S(2)}, u32[]{:S(2)}) %collective-permute-start) | collective-permute-done | bytes 278560 | tf_op jit(solution)/shard_map/ppermute | solution.py:191
  6.0 0.0 copy-start.1
  6.0 19.1 %all_to_all.20 = f32[16,32,128]{2,1,0:T(8,128)S(1)} all-to-all(f32[16,32,128]{2,1,0:T(8,128)S(1)} %bitcast.23), channel_id=1, replica_groups=mesh['xl'=2,'y'=8,'core'=2,'xh'=2,'z'=8] {'xl','y'}, dimensions={0} | all-to-all | bytes 524288 | tf_op jit(solution)/shard_map/all_to_all | solution.py:194
  25.1 0.0 copy-start
  25.1 0.9 copy-done
  26.1 1.9 %collective-permute-start.1 = (f32[512,128]{1,0:T(8,128)S(1)}, f32[512,128]{1,0:T(8,128)S(1)}, u32[]{:S(2)}, u32[]{:S(2)}) collective-permute-start(f32[512,128]{1,0:T(8,128)S(1)} %bitcast.16), channel_id=1, source_target_pairs={{0,16},{16,0},{1,17},{17,1},{2,18},{18,2},{3,19},{19,3},{4,20},{20... | collective-permute-start | bytes 786440 | tf_op jit(solution)/shard_map/ppermute | solution.py:191
  28.0 0.0 copy-done.1
  28.0 2.4 %collective-permute-start.2 = (f32[512,128]{1,0:T(8,128)S(1)}, f32[512,128]{1,0:T(8,128)S(1)}, u32[]{:S(2)}, u32[]{:S(2)}) collective-permute-start(f32[512,128]{1,0:T(8,128)S(1)} %bitcast.19), channel_id=1, source_target_pairs={{0,16},{16,0},{1,17},{17,1},{2,18},{18,2},{3,19},{19,3},{4,20},{20... | collective-permute-start | bytes 786440 | tf_op jit(solution)/shard_map/ppermute | solution.py:191
  30.4 10.2 %collective-permute-start.3 = (f32[32,128]{1,0:T(8,128)S(1)}, f32[32,128]{1,0:T(8,128)S(1)}, u32[]{:S(2)}, u32[]{:S(2)}) collective-permute-start(f32[32,128]{1,0:T(8,128)S(1)} %reduce_sum.18), channel_id=1, source_target_pairs={{0,4},{1,36},{2,68},{3,100},{4,132},{5,164},{6,196},{7,228},{8,260... | collective-permute-start | bytes 49160 | tf_op jit(solution)/shard_map/ppermute | solution.py:211
  40.6 1.4 %collective-permute-done.3 = f32[32,128]{1,0:T(8,128)S(1)} collective-permute-done((f32[32,128]{1,0:T(8,128)S(1)}, f32[32,128]{1,0:T(8,128)S(1)}, u32[]{:S(2)}, u32[]{:S(2)}) %collective-permute-start.3) | collective-permute-done | bytes 16416 | tf_op jit(solution)/shard_map/ppermute | solution.py:211
  42.0 0.0 collective-permute-done.1.green_far
  42.1 0.0 collective-permute-done.2.field_far
  42.1 21.9 %all_to_all.21 = f32[16,32,128]{2,1,0:T(8,128)S(1)} all-to-all(f32[16,32,128]{2,1,0:T(8,128)S(1)} %broadcast_in_dim.4), channel_id=1, replica_groups=mesh['xl'=2,'y'=8,'core'=2,'xh'=2,'z'=8] {'xh','z'}, dimensions={0} | all-to-all | bytes 524288 | tf_op jit(solution)/shard_map/all_to_all | solution.py:198
  64.0 1.2 %second_collide.1 = f32[512,128]{1,0:T(8,128)S(1)} custom-call(f32[512,128]{1,0:T(8,128)S(1)} %bitcast.21, f32[512,128]{1,0:T(8,128)S(1)} %bitcast.17, f32[512,128]{1,0:T(8,128)S(1)} %bitcast.20, f32[512,128]{1,0:T(8,128)S(1)} %collective-permute-done.1.green_far, f32[512,128]{1,0:T(8,128)S(1)} %collective-permute-done.2.field_far), custom_call_target="tpu_custom_call" | custom-call | tf_op jit(solution)/shard_map/second_collide/pallas_call | solution.py:166
  65.1 13.3 %all_to_all.22 = f32[16,32,128]{2,1,0:T(8,128)S(1)} all-to-all(f32[16,32,128]{2,1,0:T(8,128)S(1)} %bitcast.22), channel_id=1, replica_groups=mesh['xl'=2,'y'=8,'core'=2,'xh'=2,'z'=8] {'xl','y'}, dimensions={0} | all-to-all | bytes 524288 | tf_op jit(solution)/shard_map/all_to_all | solution.py:194
  78.4 4.2 %collective-permute-start.4 = (f32[32,128]{1,0:T(8,128)S(1)}, f32[32,128]{1,0:T(8,128)S(1)}, u32[]{:S(2)}, u32[]{:S(2)}) collective-permute-start(f32[32,128]{1,0:T(8,128)S(1)} %reduce_sum.19), channel_id=1, source_target_pairs={{0,4},{1,36},{2,68},{3,100},{4,132},{5,164},{6,196},{7,228},{8,260... | collective-permute-start | bytes 49160 | tf_op jit(solution)/shard_map/ppermute | solution.py:218
  82.6 5.5 %collective-permute-done.4 = f32[32,128]{1,0:T(8,128)S(1)} collective-permute-done((f32[32,128]{1,0:T(8,128)S(1)}, f32[32,128]{1,0:T(8,128)S(1)}, u32[]{:S(2)}, u32[]{:S(2)}) %collective-permute-start.4) | collective-permute-done | bytes 16416 | tf_op jit(solution)/shard_map/ppermute | solution.py:218
  88.1 16.3 %all_to_all.23 = f32[16,32,128]{2,1,0:T(8,128)S(1)} all-to-all(f32[16,32,128]{2,1,0:T(8,128)S(1)} %broadcast_in_dim.5), channel_id=1, replica_groups=mesh['xl'=2,'y'=8,'core'=2,'xh'=2,'z'=8] {'xh','z'}, dimensions={0} | all-to-all | bytes 524288 | tf_op jit(solution)/shard_map/all_to_all | solution.py:198
  104.4 0.7 copy.7
  (7 shorter events, 0.1 us)
Async XLA Ops:
  2.5 3.5 %collective-permute-start = (f32[544,128]{1,0:T(8,128)S(1)}, f32[544,128]{1,0:T(8,128)S(1)}, u32[]{:S(2)}, u32[]{:S(2)}) collective-permute-start(f32[544,128]{1,0:T(8,128)S(1)} %get-tuple-element.17), channel_id=1, source_target_pairs={{0,16},{16,0},{1,17},{17,1},{2,18},{18,2},{3,19},{19,3},{4,20},{20... | collective-permute-start | bytes 835592 | tf_op jit(solution)/shard_map/ppermute | solution.py:191
  6.0 22.0 %copy-start.1 = (f32[8,16,2,256]{3,2,1,0:T(2,128)S(1)}, f32[8,16,2,256]{3,2,1,0:T(2,128)}, u32[]{:S(2)}) copy-start(f32[8,16,2,256]{3,2,1,0:T(2,128)} %param.5) | copy-start | bytes 786436
  25.1 1.0 copy-start
  26.1 16.0 %collective-permute-start.1 = (f32[512,128]{1,0:T(8,128)S(1)}, f32[512,128]{1,0:T(8,128)S(1)}, u32[]{:S(2)}, u32[]{:S(2)}) collective-permute-start(f32[512,128]{1,0:T(8,128)S(1)} %bitcast.16), channel_id=1, source_target_pairs={{0,16},{16,0},{1,17},{17,1},{2,18},{18,2},{3,19},{19,3},{4,20},{20... | collective-permute-start | bytes 786440 | tf_op jit(solution)/shard_map/ppermute | solution.py:191
  28.0 14.1 %collective-permute-start.2 = (f32[512,128]{1,0:T(8,128)S(1)}, f32[512,128]{1,0:T(8,128)S(1)}, u32[]{:S(2)}, u32[]{:S(2)}) collective-permute-start(f32[512,128]{1,0:T(8,128)S(1)} %bitcast.19), channel_id=1, source_target_pairs={{0,16},{16,0},{1,17},{17,1},{2,18},{18,2},{3,19},{19,3},{4,20},{20... | collective-permute-start | bytes 786440 | tf_op jit(solution)/shard_map/ppermute | solution.py:191
  30.4 11.6 %collective-permute-start.3 = (f32[32,128]{1,0:T(8,128)S(1)}, f32[32,128]{1,0:T(8,128)S(1)}, u32[]{:S(2)}, u32[]{:S(2)}) collective-permute-start(f32[32,128]{1,0:T(8,128)S(1)} %reduce_sum.18), channel_id=1, source_target_pairs={{0,4},{1,36},{2,68},{3,100},{4,132},{5,164},{6,196},{7,228},{8,260... | collective-permute-start | bytes 49160 | tf_op jit(solution)/shard_map/ppermute | solution.py:211
  78.4 9.7 %collective-permute-start.4 = (f32[32,128]{1,0:T(8,128)S(1)}, f32[32,128]{1,0:T(8,128)S(1)}, u32[]{:S(2)}, u32[]{:S(2)}) collective-permute-start(f32[32,128]{1,0:T(8,128)S(1)} %reduce_sum.19), channel_id=1, source_target_pairs={{0,4},{1,36},{2,68},{3,100},{4,132},{5,164},{6,196},{7,228},{8,260... | collective-permute-start | bytes 49160 | tf_op jit(solution)/shard_map/ppermute | solution.py:218
where the time goes:
time: 106 us; the launch traced here: 105 us
  blocking collectives  70.5 us (67%)
  starting transfers between devices  20.7 us (20%)
  waiting for transfers between devices  8.43 us (8%)
  Pallas kernels  3.64 us (3%)
  local copies, waits for them, and re-layouts  1.67 us (2%)
    all_to_all x2, blocking collectives, gathered(): return lax.all_to_all(copies, B, 0, 0, tiled=True).reshape(rows, width)  38.1 us
    all_to_all x2, blocking collectives, reduced(): lax.all_to_all(partial_sum.reshape(fronts, -1, width), A, 0, 0, tiled=True)  32.4 us
    ppermute x1, starting transfers between devices, corrector(): turned = lax.ppermute(piece, EVERY, turns[0])  10.2 us
    ppermute x3, starting transfers between devices, swap(): return lax.ppermute(value, 'core', [(0, 1), (1, 0)])  6.24 us
    ppermute x1, waiting for transfers between devices, corrector(): turned = lax.ppermute(reduced(image), EVERY, turns[1])  5.49 us
    ppermute x1, starting transfers between devices, corrector(): turned = lax.ppermute(reduced(image), EVERY, turns[1])  4.21 us
    pallas_call x1, Pallas kernels, first_collide(): pl.pallas_call(functools.partial(first_kernel, orbits, order), out_shape=...  2.48 us
  transfers between devices with their start and end apart: 5, of which 3 were waited for; matrix products, arithmetic and copies ran while one was open for 0% of the time, Pallas kernels for 0%

commit v1 on v0

--- a/solution.py
+++ b/solution.py
@@ -19,13 +19,6 @@
     high = value.astype(jnp.bfloat16)
     low = (value - high.astype(jnp.float32)).astype(jnp.bfloat16)
     return high, low
-
-
-def dot3(left, right):
-    def one(x, y):
-        return jnp.dot(x, y, preferred_element_type=jnp.float32)
-
-    return one(left[0], right[0]) + (one(left[0], right[1]) + one(left[1], right[0]))
 
 
 def swap_orbitals(value, orbits):
@@ -64,12 +57,18 @@
 
 
 def image_of(left_re, left_im, refs):
-    left_re, left_im = split(left_re), split(left_im)
+    (re_high, re_low), (im_high, im_low) = split(left_re), split(left_im)
     right_re, right_im = split(history(refs, 0)), split(history(refs, 1))
-    return (
-        dot3(left_re, right_re) - dot3(left_im, right_im),
-        dot3(left_re, right_im) + dot3(left_im, right_re),
-    )
+
+    def one(re_first, im_first, first, second):
+        left = jnp.concatenate(
+            [re_first[0], im_first[0], re_first[0], im_first[0], re_first[1], im_first[1]], axis=1)
+        right = jnp.concatenate(
+            [first[0], second[0], first[1], second[1], first[0], second[0]], axis=0)
+        return jnp.dot(left, right, preferred_element_type=jnp.float32)
+
+    re, im = (re_high, re_low), (im_high, im_low)
+    return one(re, (-im_high, -im_low), right_re, right_im), one(re, im, right_im, right_re)
 
 
 def put(target_ref, part, image, orbits, order):
@@ -90,7 +89,7 @@
     ]
     for copy in copies:
         copy.start()
-    core, xh, z = (lax.axis_index(axis) for axis in ("core", "xh", "z"))
+    core, xl, xh, z = (lax.axis_index(axis) for axis in ("core", "xl", "xh", "z"))
     fronts = len(order)
     piece = 2 * orbits
     rows = init.shape[0]
@@ -100,7 +99,7 @@
 
     copies[0].wait()
     near_ref[...] = front(core * fronts + z)
-    last_ref[...] = front(xh * fronts + z)
+    last_ref[...] = front((core + 1 + xh + xl) % 2 * fronts + z)
     other_ref[rows:, :] = front((1 - core) * fronts + z)
     re = init[pl.ds(0, rows // 2, stride=2), :]
     im = init[pl.ds(1, rows // 2, stride=2), :]
@@ -136,8 +135,12 @@
     images = image_of(
         jnp.concatenate(left_re, axis=1), jnp.concatenate(left_im, axis=1),
         (green_ref, field_ref, green_far, field_far))
+    lanes = out_ref.shape[1]
+    straight = (core + 1 + lax.axis_index("xh")) % 2 == 0
     for part, image in enumerate(images):
-        put(out_ref, part, image, orbits, order)
+        low, high = image[:, :lanes], image[:, lanes:]
+        first, second = jnp.where(straight, low, high), jnp.where(straight, high, low)
+        put(out_ref, part, jnp.concatenate([first, second], axis=1), orbits, order)
 
 
 VMEM = pl.BlockSpec(memory_space=pltpu.VMEM)
@@ -216,7 +219,9 @@
     current = gathered(copies)
     image = second_collide(current, (green, field, green_far, field_far), orbits, order)
     turned = lax.ppermute(reduced(image), EVERY, turns[1])
-    return gathered(copies_of(last, turned)).reshape(front_init.shape)
+    final = gathered(copies_of(last, turned)).reshape(2, rows // 2, width)
+    straight = (lax.axis_index("core") + 1 + lax.axis_index("xl")) % 2 == 0
+    return jnp.where(straight, final, final[::-1]).reshape(front_init.shape)
 
 
 def solution(mesh):
@@ -234,7 +239,7 @@
     turns = [
         [(place(xl, y, core, xh, z), place(xh, z, core, xl, (y + zs // 2) % zs))
          for xl, y, core, xh, z in everyone],
-        [(place(xl, y, core, xh, z), place(xh, z, xl, core, (y + zs // 2) % zs))
+        [(place(xl, y, core, xh, z), place(xh, z, core if xl != xh else 1 - core, xl, (y + zs // 2) % zs))
          for xl, y, core, xh, z in everyone],
     ]
     return jax.shard_map(

time: 106 us -> 105 us (level)
  blocking collectives: 70.5 us -> 54.2 us
  waiting for transfers between devices: 8.43 us -> 20.4 us
  starting transfers between devices: 20.7 us -> 24.1 us
    all_to_all x2 -> x1, blocking collectives: 38.1 us -> 21.9 us  [gathered(): return lax.all_to_all(copies, B, 0, 0, tiled=True).reshape(rows, width)]
    all_to_all x0 -> x1, waiting for transfers between devices: none -> 10.4 us  [gathered(): return lax.all_to_all(copies, B, 0, 0, tiled=True).reshape(rows, width)]
    all_to_all x0 -> x1, starting transfers between devices: none -> 5.76 us  [gathered(): return lax.all_to_all(copies, B, 0, 0, tiled=True).reshape(rows, width)]
    ppermute x1, starting transfers between devices: 4.21 us -> 1.92 us  [corrector(): turned = lax.ppermute(reduced(image), EVERY, turns[1])]
    ppermute x1, waiting for transfers between devices: 5.49 us -> 7.04 us  [corrector(): turned = lax.ppermute(reduced(image), EVERY, turns[1])]
  transfers between devices with their start and end apart: 5 -> 6, of which waited for: 3 -> 4; matrix products, arithmetic and copies ran while one was open for 0% -> 0% of each run, Pallas kernels for 0% -> 0%
where the time goes in v1:
time: 105 us
  blocking collectives  54.2 us (52%)
  starting transfers between devices  24.1 us (23%)
  waiting for transfers between devices  20.4 us (19%)
  Pallas kernels  3.58 us (3%)
  local copies, waits for them, and re-layouts  1.68 us (2%)
    all_to_all x2, blocking collectives, reduced(): lax.all_to_all(partial_sum.reshape(fronts, -1, width), A, 0, 0, tiled=True)  32.4 us
    all_to_all x1, blocking collectives, gathered(): return lax.all_to_all(copies, B, 0, 0, tiled=True).reshape(rows, width)  21.9 us
    all_to_all x1, waiting for transfers between devices, gathered(): return lax.all_to_all(copies, B, 0, 0, tiled=True).reshape(rows, width)  10.4 us
    ppermute x1, starting transfers between devices, corrector(): turned = lax.ppermute(piece, EVERY, turns[0])  10.2 us
    ppermute x1, waiting for transfers between devices, corrector(): turned = lax.ppermute(reduced(image), EVERY, turns[1])  7.04 us
    ppermute x3, starting transfers between devices, swap(): return lax.ppermute(value, 'core', [(0, 1), (1, 0)])  6.24 us
    all_to_all x1, starting transfers between devices, gathered(): return lax.all_to_all(copies, B, 0, 0, tiled=True).reshape(rows, width)  5.76 us
    pallas_call x1, Pallas kernels, first_collide(): pl.pallas_call(functools.partial(first_kernel, orbits, order), out_shape=...  2.48 us
  transfers between devices with their start and end apart: 6, of which 4 were waited for; matrix products, arithmetic and copies ran while one was open for 0% of the time, Pallas kernels for 0%

profile of v1, /device:TPU:8, one launch (start us, length us, event | category | flops | bytes accessed | tf_op | source)
XLA Modules:
  0.0 104.9 jit_solution(206678683827221514)
XLA Ops:
  0.0 2.5 %first_collide.1 = (f32[512,128]{1,0:T(8,128)S(1)}, f32[544,128]{1,0:T(8,128)S(1)}, f32[32,128]{1,0:T(8,128)S(1)}, f32[32,128]{1,0:T(8,128)S(1)}) custom-call(f32[512,128]{1,0:T(8,128)} %bitcast.26, f32[512,128]{1,0:T(8,128)} %bitcast.16, f32[512,128]{1,0:T(8,128)} %bitcast.19), custom_call_target="tpu_custom_call" | custom-call | tf_op jit(solution)/shard_map/first_collide/pallas_call | solution.py:153
  2.5 1.9 %collective-permute-start = (f32[544,128]{1,0:T(8,128)S(1)}, f32[544,128]{1,0:T(8,128)S(1)}, u32[]{:S(2)}, u32[]{:S(2)}) collective-permute-start(f32[544,128]{1,0:T(8,128)S(1)} %get-tuple-element.17), channel_id=1, source_target_pairs={{0,16},{16,0},{1,17},{17,1},{2,18},{18,2},{3,19},{19,3},{4,20},{20... | collective-permute-start | bytes 835592 | tf_op jit(solution)/shard_map/ppermute | solution.py:194
  4.4 1.5 %collective-permute-done = f32[544,128]{1,0:T(8,128)S(1)} collective-permute-done((f32[544,128]{1,0:T(8,128)S(1)}, f32[544,128]{1,0:T(8,128)S(1)}, u32[]{:S(2)}, u32[]{:S(2)}) %collective-permute-start) | collective-permute-done | bytes 278560 | tf_op jit(solution)/shard_map/ppermute | solution.py:194
  6.0 0.0 copy-start.1
  6.0 19.1 %all_to_all.20 = f32[16,32,128]{2,1,0:T(8,128)S(1)} all-to-all(f32[16,32,128]{2,1,0:T(8,128)S(1)} %bitcast.24), channel_id=1, replica_groups=mesh['xl'=2,'y'=8,'core'=2,'xh'=2,'z'=8] {'xl','y'}, dimensions={0} | all-to-all | bytes 524288 | tf_op jit(solution)/shard_map/all_to_all | solution.py:197
  25.1 0.0 copy-start
  25.1 0.9 copy-done
  26.1 1.9 %collective-permute-start.1 = (f32[512,128]{1,0:T(8,128)S(1)}, f32[512,128]{1,0:T(8,128)S(1)}, u32[]{:S(2)}, u32[]{:S(2)}) collective-permute-start(f32[512,128]{1,0:T(8,128)S(1)} %bitcast.17), channel_id=1, source_target_pairs={{0,16},{16,0},{1,17},{17,1},{2,18},{18,2},{3,19},{19,3},{4,20},{20... | collective-permute-start | bytes 786440 | tf_op jit(solution)/shard_map/ppermute | solution.py:194
  28.0 0.0 copy-done.1
  28.0 2.4 %collective-permute-start.2 = (f32[512,128]{1,0:T(8,128)S(1)}, f32[512,128]{1,0:T(8,128)S(1)}, u32[]{:S(2)}, u32[]{:S(2)}) collective-permute-start(f32[512,128]{1,0:T(8,128)S(1)} %bitcast.20), channel_id=1, source_target_pairs={{0,16},{16,0},{1,17},{17,1},{2,18},{18,2},{3,19},{19,3},{4,20},{20... | collective-permute-start | bytes 786440 | tf_op jit(solution)/shard_map/ppermute | solution.py:194
  30.4 10.2 %collective-permute-start.3 = (f32[32,128]{1,0:T(8,128)S(1)}, f32[32,128]{1,0:T(8,128)S(1)}, u32[]{:S(2)}, u32[]{:S(2)}) collective-permute-start(f32[32,128]{1,0:T(8,128)S(1)} %reduce_sum.18), channel_id=1, source_target_pairs={{0,4},{1,36},{2,68},{3,100},{4,132},{5,164},{6,196},{7,228},{8,260... | collective-permute-start | bytes 49160 | tf_op jit(solution)/shard_map/ppermute | solution.py:214
  40.6 1.4 %collective-permute-done.3 = f32[32,128]{1,0:T(8,128)S(1)} collective-permute-done((f32[32,128]{1,0:T(8,128)S(1)}, f32[32,128]{1,0:T(8,128)S(1)}, u32[]{:S(2)}, u32[]{:S(2)}) %collective-permute-start.3) | collective-permute-done | bytes 16416 | tf_op jit(solution)/shard_map/ppermute | solution.py:214
  42.0 0.0 collective-permute-done.1.green_far
  42.1 0.0 collective-permute-done.2.field_far
  42.1 21.9 %all_to_all.21 = f32[16,32,128]{2,1,0:T(8,128)S(1)} all-to-all(f32[16,32,128]{2,1,0:T(8,128)S(1)} %broadcast_in_dim.4), channel_id=1, replica_groups=mesh['xl'=2,'y'=8,'core'=2,'xh'=2,'z'=8] {'xh','z'}, dimensions={0} | all-to-all | bytes 524288 | tf_op jit(solution)/shard_map/all_to_all | solution.py:201
  64.0 1.1 %second_collide.1 = f32[512,128]{1,0:T(8,128)S(1)} custom-call(f32[512,128]{1,0:T(8,128)S(1)} %bitcast.22, f32[512,128]{1,0:T(8,128)S(1)} %bitcast.18, f32[512,128]{1,0:T(8,128)S(1)} %bitcast.21, f32[512,128]{1,0:T(8,128)S(1)} %collective-permute-done.1.green_far, f32[512,128]{1,0:T(8,128)S(1)} %collective-permute-done.2.field_far), custom_call_target="tpu_custom_call" | custom-call | tf_op jit(solution)/shard_map/second_collide/pallas_call | solution.py:169
  65.1 13.3 %all_to_all.22 = f32[16,32,128]{2,1,0:T(8,128)S(1)} all-to-all(f32[16,32,128]{2,1,0:T(8,128)S(1)} %bitcast.23), channel_id=1, replica_groups=mesh['xl'=2,'y'=8,'core'=2,'xh'=2,'z'=8] {'xl','y'}, dimensions={0} | all-to-all | bytes 524288 | tf_op jit(solution)/shard_map/all_to_all | solution.py:197
  78.3 1.9 %collective-permute-start.4 = (f32[32,128]{1,0:T(8,128)S(1)}, f32[32,128]{1,0:T(8,128)S(1)}, u32[]{:S(2)}, u32[]{:S(2)}) collective-permute-start(f32[32,128]{1,0:T(8,128)S(1)} %reduce_sum.19), channel_id=1, source_target_pairs={{0,20},{1,52},{2,84},{3,116},{4,148},{5,180},{6,212},{7,244},{8,26... | collective-permute-start | bytes 49160 | tf_op jit(solution)/shard_map/ppermute | solution.py:221
  80.3 7.0 %collective-permute-done.4 = f32[32,128]{1,0:T(8,128)S(1)} collective-permute-done((f32[32,128]{1,0:T(8,128)S(1)}, f32[32,128]{1,0:T(8,128)S(1)}, u32[]{:S(2)}, u32[]{:S(2)}) %collective-permute-start.4) | collective-permute-done | bytes 16416 | tf_op jit(solution)/shard_map/ppermute | solution.py:221
  87.3 0.7 broadcast_in_dim.5
  88.0 5.8 %all-to-all-start.3 = ((f32[16,32,128]{2,1,0:T(8,128)}), f32[16,32,128]{2,1,0:T(8,128)S(1)}, u32[]{:S(2)}, u32[]{:S(2)}) async-start(f32[16,32,128]{2,1,0:T(8,128)} %broadcast_in_dim.5), calls=%async_computation.3 | async-start | bytes 524288 | tf_op jit(solution)/shard_map/all_to_all | solution.py:201
  93.8 10.4 %all-to-all-done.3 = f32[16,32,128]{2,1,0:T(8,128)S(1)} async-done(((f32[16,32,128]{2,1,0:T(8,128)}), f32[16,32,128]{2,1,0:T(8,128)S(1)}, u32[]{:S(2)}, u32[]{:S(2)}) %all-to-all-start.3) | async-done | bytes 262176 | tf_op jit(solution)/shard_map/all_to_all | solution.py:201
  104.2 0.7 reverse_select_fusion
  (6 shorter events, 0.1 us)
Async XLA Ops:
  2.5 3.5 %collective-permute-start = (f32[544,128]{1,0:T(8,128)S(1)}, f32[544,128]{1,0:T(8,128)S(1)}, u32[]{:S(2)}, u32[]{:S(2)}) collective-permute-start(f32[544,128]{1,0:T(8,128)S(1)} %get-tuple-element.17), channel_id=1, source_target_pairs={{0,16},{16,0},{1,17},{17,1},{2,18},{18,2},{3,19},{19,3},{4,20},{20... | collective-permute-start | bytes 835592 | tf_op jit(solution)/shard_map/ppermute | solution.py:194
  6.0 22.0 %copy-start.1 = (f32[8,16,2,256]{3,2,1,0:T(2,128)S(1)}, f32[8,16,2,256]{3,2,1,0:T(2,128)}, u32[]{:S(2)}) copy-start(f32[8,16,2,256]{3,2,1,0:T(2,128)} %param.5) | copy-start | bytes 786436
  25.1 1.0 copy-start
  26.1 16.0 %collective-permute-start.1 = (f32[512,128]{1,0:T(8,128)S(1)}, f32[512,128]{1,0:T(8,128)S(1)}, u32[]{:S(2)}, u32[]{:S(2)}) collective-permute-start(f32[512,128]{1,0:T(8,128)S(1)} %bitcast.17), channel_id=1, source_target_pairs={{0,16},{16,0},{1,17},{17,1},{2,18},{18,2},{3,19},{19,3},{4,20},{20... | collective-permute-start | bytes 786440 | tf_op jit(solution)/shard_map/ppermute | solution.py:194
  28.0 14.1 %collective-permute-start.2 = (f32[512,128]{1,0:T(8,128)S(1)}, f32[512,128]{1,0:T(8,128)S(1)}, u32[]{:S(2)}, u32[]{:S(2)}) collective-permute-start(f32[512,128]{1,0:T(8,128)S(1)} %bitcast.20), channel_id=1, source_target_pairs={{0,16},{16,0},{1,17},{17,1},{2,18},{18,2},{3,19},{19,3},{4,20},{20... | collective-permute-start | bytes 786440 | tf_op jit(solution)/shard_map/ppermute | solution.py:194
  30.4 11.6 %collective-permute-start.3 = (f32[32,128]{1,0:T(8,128)S(1)}, f32[32,128]{1,0:T(8,128)S(1)}, u32[]{:S(2)}, u32[]{:S(2)}) collective-permute-start(f32[32,128]{1,0:T(8,128)S(1)} %reduce_sum.18), channel_id=1, source_target_pairs={{0,4},{1,36},{2,68},{3,100},{4,132},{5,164},{6,196},{7,228},{8,260... | collective-permute-start | bytes 49160 | tf_op jit(solution)/shard_map/ppermute | solution.py:214
  78.3 9.0 %collective-permute-start.4 = (f32[32,128]{1,0:T(8,128)S(1)}, f32[32,128]{1,0:T(8,128)S(1)}, u32[]{:S(2)}, u32[]{:S(2)}) collective-permute-start(f32[32,128]{1,0:T(8,128)S(1)} %reduce_sum.19), channel_id=1, source_target_pairs={{0,20},{1,52},{2,84},{3,116},{4,148},{5,180},{6,212},{7,244},{8,26... | collective-permute-start | bytes 49160 | tf_op jit(solution)/shard_map/ppermute | solution.py:221
  88.0 16.2 %all-to-all-start.3 = ((f32[16,32,128]{2,1,0:T(8,128)}), f32[16,32,128]{2,1,0:T(8,128)S(1)}, u32[]{:S(2)}, u32[]{:S(2)}) async-start(f32[16,32,128]{2,1,0:T(8,128)} %broadcast_in_dim.5), calls=%async_computation.3 | async-start | bytes 524288 | tf_op jit(solution)/shard_map/all_to_all | solution.py:201

commit v2 on v1

--- a/solution.py
+++ b/solution.py
@@ -80,8 +80,21 @@
                 front * orbits:(front + 1) * orbits, half * lanes:(half + 1) * lanes]
 
 
+def half_image(init_ref, green_ref, field_ref, orbits, lower):
+    pairs = init_ref.shape[0] // 4
+    re, im = (
+        jnp.where(lower, init_ref[pl.ds(part, pairs, stride=2), :],
+                  init_ref[pl.ds(2 * pairs + part, pairs, stride=2), :])
+        for part in range(2)
+    )
+    sigma_re, sigma_im = sigma_pair(re, im, orbits)
+    return image_of(
+        jnp.concatenate([sigma_re, re], axis=1), jnp.concatenate([sigma_im, im], axis=1),
+        (green_ref, field_ref))
+
+
 def first_kernel(orbits, order, init_ref, green_ref, field_ref,
-                 own_ref, other_ref, near_ref, last_ref, init, green, field, sems):
+                 other_ref, near_ref, last_ref, flag_ref, init, green, field, sems):
     copies = [
         pltpu.make_async_copy(source, target, sems.at[n])
         for n, (source, target) in enumerate(
@@ -93,27 +106,24 @@
     fronts = len(order)
     piece = 2 * orbits
     rows = init.shape[0]
+    flag_ref[...] = jnp.full(flag_ref.shape, (core + 1 + xl) % 2, jnp.int32)
 
     def front(index):
         return init[pl.ds(pl.multiple_of(index * piece, piece), piece), :]
 
-    copies[0].wait()
+    for copy in copies:
+        copy.wait()
     near_ref[...] = front(core * fronts + z)
     last_ref[...] = front((core + 1 + xh + xl) % 2 * fronts + z)
     other_ref[rows:, :] = front((1 - core) * fronts + z)
-    re = init[pl.ds(0, rows // 2, stride=2), :]
-    im = init[pl.ds(1, rows // 2, stride=2), :]
-    sigma_re, sigma_im = sigma_pair(re, im, orbits)
-    left_re = jnp.concatenate([sigma_re, re], axis=1)
-    left_im = jnp.concatenate([sigma_im, im], axis=1)
-    copies[1].wait()
-    copies[2].wait()
-    images = image_of(left_re, left_im, (green, field))
-    cut = rows // 4
-    for part, image in enumerate(images):
-        low, high = image[:cut], image[cut:]
-        put(own_ref, part, jnp.where(core == 0, low, high), orbits, order)
-        put(other_ref, part, jnp.where(core == 0, high, low), orbits, order)
+    for part, image in enumerate(half_image(init, green, field, orbits, core == 1)):
+        put(other_ref, part, image, orbits, order)
+
+
+def kept_kernel(orbits, order, init_ref, green_ref, field_ref, own_ref):
+    core = lax.axis_index("core")
+    for part, image in enumerate(half_image(init_ref, green_ref, field_ref, orbits, core == 0)):
+        put(own_ref, part, image, orbits, order)
 
 
 def second_kernel(orbits, order, front_ref, green_ref, field_ref, green_far, field_far, out_ref):
@@ -153,16 +163,29 @@
     return pl.pallas_call(
         functools.partial(first_kernel, orbits, order),
         out_shape=[
-            jax.ShapeDtypeStruct((n, width), jnp.float32)
-            for n in (rows, rows + 2 * orbits, 2 * orbits, 2 * orbits)
+            jax.ShapeDtypeStruct((n, width), kind) for n, kind in (
+                (rows + 2 * orbits, jnp.float32), (2 * orbits, jnp.float32),
+                (2 * orbits, jnp.float32), (8, jnp.int32), (rows, jnp.float32),
+                (rows, jnp.float32), (rows, jnp.float32))
         ],
         in_specs=[pl.BlockSpec(memory_space=pltpu.HBM)] * 3,
-        out_specs=[VMEM] * 4,
-        scratch_shapes=[pltpu.VMEM(x.shape, x.dtype) for x in (init, green, field)]
-        + [pltpu.SemaphoreType.DMA((3,))],
+        out_specs=[VMEM] * 7,
+        scratch_shapes=[pltpu.SemaphoreType.DMA((3,))],
         compiler_params=LIMIT,
         name="first_collide",
     )(*operands)
+
+
+def kept_collide(init, green, field, orbits, order):
+    return pl.pallas_call(
+        functools.partial(kept_kernel, orbits, order),
+        out_shape=jax.ShapeDtypeStruct(init.shape, jnp.float32),
+        in_specs=[VMEM] * 3,
+        out_specs=VMEM,
+        compiler_params=LIMIT,
+        cost_estimate=pl.CostEstimate(flops=10**8, bytes_accessed=10**6, transcendentals=0),
+        name="kept_collide",
+    )(init, green, field)
 
 
 def second_collide(front, histories, orbits, order):
@@ -206,8 +229,12 @@
 
     green, field = tiles(green_hist), tiles(field_hist)
     order = [(y + zs // 2) % zs for y in range(ys)]
-    own, other, near, last = first_collide(init, green, field, orbits, order)
+    other, near, last, flag, init, green, field = first_collide(
+        init, green, field, orbits, order)
     arrived = swap(other)
+    own = kept_collide(init, green, field, orbits, order)
+    flag = jnp.broadcast_to(flag == 0, (2, rows // 16, 8, width))
+    own, flag = lax.optimization_barrier((own, flag))
     piece = reduced(own + arrived[:rows])
     near = jnp.where(lax.axis_index("xh") == lax.axis_index("core"), near, arrived[rows:])
     green_late, field_late, piece = lax.optimization_barrier((green, field, piece))
@@ -219,9 +246,8 @@
     current = gathered(copies)
     image = second_collide(current, (green, field, green_far, field_far), orbits, order)
     turned = lax.ppermute(reduced(image), EVERY, turns[1])
-    final = gathered(copies_of(last, turned)).reshape(2, rows // 2, width)
-    straight = (lax.axis_index("core") + 1 + lax.axis_index("xl")) % 2 == 0
-    return jnp.where(straight, final, final[::-1]).reshape(front_init.shape)
+    final = gathered(copies_of(last, turned)).reshape(2, -1, 8, width)
+    return jnp.where(flag, final, final[::-1]).reshape(front_init.shape)
 
 
 def solution(mesh):

time: 105 us -> 103 us (0.981)
  blocking collectives: 54.2 us -> 70.1 us
  waiting for transfers between devices: 20.4 us -> 9.23 us
  starting transfers between devices: 24.1 us -> 18.4 us
  local copies, waits for them, and re-layouts: 1.68 us -> 0.06 us
    all_to_all x1 -> x2, blocking collectives: 21.9 us -> 37.8 us  [gathered(): return lax.all_to_all(copies, B, 0, 0, tiled=True).reshape(rows, width)]
    all_to_all x1 -> x0, waiting for transfers between devices: 10.4 us -> none  [gathered(): return lax.all_to_all(copies, B, 0, 0, tiled=True).reshape(rows, width)]
    all_to_all x1 -> x0, starting transfers between devices: 5.76 us -> none  [gathered(): return lax.all_to_all(copies, B, 0, 0, tiled=True).reshape(rows, width)]
  transfers between devices with their start and end apart: 6 -> 5, of which waited for: 4 -> 3; matrix products, arithmetic and copies ran while one was open for 0% -> 0% of each run, Pallas kernels for 0% -> 1%
where the time goes in v2:
time: 103 us; the launch traced here: 102 us
  blocking collectives  70.1 us (68%)
  starting transfers between devices  18.4 us (18%)
  waiting for transfers between devices  9.23 us (9%)
  Pallas kernels  3.64 us (4%)
    all_to_all x2, blocking collectives, gathered(): return lax.all_to_all(copies, B, 0, 0, tiled=True).reshape(rows, width)  37.8 us
    all_to_all x2, blocking collectives, reduced(): lax.all_to_all(partial_sum.reshape(fronts, -1, width), A, 0, 0, tiled=True)  32.2 us
    ppermute x1, starting transfers between devices, corrector(): turned = lax.ppermute(piece, EVERY, turns[0])  10.2 us
    ppermute x1, waiting for transfers between devices, corrector(): turned = lax.ppermute(reduced(image), EVERY, turns[1])  7.04 us
    ppermute x3, starting transfers between devices, swap(): return lax.ppermute(value, 'core', [(0, 1), (1, 0)])  6.25 us
  transfers between devices with their start and end apart: 5, of which 3 were waited for; matrix products, arithmetic and copies ran while one was open for 0% of the time, Pallas kernels for 1%

profile of v2, /device:TPU:8, one launch (start us, length us, event | category | flops | bytes accessed | tf_op | source)
XLA Modules:
  0.0 102.3 jit_solution(17595829307168190347)
XLA Ops:
  0.0 1.8 %first_collide.1 = (f32[544,128]{1,0:T(8,128)S(1)}, f32[32,128]{1,0:T(8,128)S(1)}, f32[32,128]{1,0:T(8,128)S(1)}, s32[8,128]{1,0:T(8,128)S(1)}, f32[512,128]{1,0...) custom-call(f32[512,128]{1,0:T(8,128)} %bitcast.20, f32[512,128]{1,0:T(8,128)} %bitcast.21, f32[512,128]{1,0:T(8,128)} %bitcast.22), custom_call_target="tpu_custom_call" | custom-call | tf_op jit(solution)/shard_map/first_collide/pallas_call | solution.py:163
  1.8 1.9 %collective-permute-start = (f32[544,128]{1,0:T(8,128)S(1)}, f32[544,128]{1,0:T(8,128)S(1)}, u32[]{:S(2)}, u32[]{:S(2)}) collective-permute-start(f32[544,128]{1,0:T(8,128)S(1)} %get-tuple-element.27), channel_id=1, source_target_pairs={{0,16},{16,0},{1,17},{17,1},{2,18},{18,2},{3,19},{19,3},{4,20},{20... | collective-permute-start | bytes 835592 | tf_op jit(solution)/shard_map/ppermute | solution.py:217
  3.8 0.7 kept_collide.1
  4.5 0.8 collective-permute-done
  5.3 19.0 %all_to_all.20 = f32[16,32,128]{2,1,0:T(8,128)S(1)} all-to-all(f32[16,32,128]{2,1,0:T(8,128)S(1)} %bitcast.18), channel_id=1, replica_groups=mesh['xl'=2,'y'=8,'core'=2,'xh'=2,'z'=8] {'xl','y'}, dimensions={0} | all-to-all | bytes 524288 | tf_op jit(solution)/shard_map/all_to_all | solution.py:220
  24.3 1.9 %collective-permute-start.1 = (f32[512,128]{1,0:T(8,128)S(1)}, f32[512,128]{1,0:T(8,128)S(1)}, u32[]{:S(2)}, u32[]{:S(2)}) collective-permute-start(f32[512,128]{1,0:T(8,128)S(1)} %get-tuple-element.28.green_ref), channel_id=1, source_target_pairs={{0,16},{16,0},{1,17},{17,1},{2,18},{18,2},{3,19},{19,3},{4,20},{20... | collective-permute-start | bytes 786440 | tf_op jit(solution)/shard_map/ppermute | solution.py:217
  26.3 2.4 %collective-permute-start.2 = (f32[512,128]{1,0:T(8,128)S(1)}, f32[512,128]{1,0:T(8,128)S(1)}, u32[]{:S(2)}, u32[]{:S(2)}) collective-permute-start(f32[512,128]{1,0:T(8,128)S(1)} %get-tuple-element.29.field_ref), channel_id=1, source_target_pairs={{0,16},{16,0},{1,17},{17,1},{2,18},{18,2},{3,19},{19,3},{4,20},{20... | collective-permute-start | bytes 786440 | tf_op jit(solution)/shard_map/ppermute | solution.py:217
  28.7 10.2 %collective-permute-start.3 = (f32[32,128]{1,0:T(8,128)S(1)}, f32[32,128]{1,0:T(8,128)S(1)}, u32[]{:S(2)}, u32[]{:S(2)}) collective-permute-start(f32[32,128]{1,0:T(8,128)S(1)} %reduce_sum.18), channel_id=1, source_target_pairs={{0,4},{1,36},{2,68},{3,100},{4,132},{5,164},{6,196},{7,228},{8,260... | collective-permute-start | bytes 49160 | tf_op jit(solution)/shard_map/ppermute | solution.py:241
  38.9 1.4 %collective-permute-done.3 = f32[32,128]{1,0:T(8,128)S(1)} collective-permute-done((f32[32,128]{1,0:T(8,128)S(1)}, f32[32,128]{1,0:T(8,128)S(1)}, u32[]{:S(2)}, u32[]{:S(2)}) %collective-permute-start.3) | collective-permute-done | bytes 16416 | tf_op jit(solution)/shard_map/ppermute | solution.py:241
  40.3 0.0 collective-permute-done.1.green_far
  40.3 0.0 collective-permute-done.2.field_far
  40.4 21.9 %all_to_all.21 = f32[16,32,128]{2,1,0:T(8,128)S(1)} all-to-all(f32[16,32,128]{2,1,0:T(8,128)S(1)} %broadcast_in_dim.7), channel_id=1, replica_groups=mesh['xl'=2,'y'=8,'core'=2,'xh'=2,'z'=8] {'xh','z'}, dimensions={0} | all-to-all | bytes 524288 | tf_op jit(solution)/shard_map/all_to_all | solution.py:224
  62.2 1.1 %second_collide.1 = f32[512,128]{1,0:T(8,128)S(1)} custom-call(f32[512,128]{1,0:T(8,128)S(1)} %bitcast.16, f32[512,128]{1,0:T(8,128)S(1)} %get-tuple-element.28.green_ref, f32[512,128]{1,0:T(8,128)S(1)} %get-tuple-element.29.field_ref, f32[512,128]{1,0:T(8,128)S(1)} %collective-permute-done.1.green_far, f32[512,128]{1,0:T(8,128)S(1)} %collective-permute-done.2.field_far), custom_call_target="tpu_custom_call" | custom-call | tf_op jit(solution)/shard_map/second_collide/pallas_call | solution.py:192
  63.3 13.3 %all_to_all.22 = f32[16,32,128]{2,1,0:T(8,128)S(1)} all-to-all(f32[16,32,128]{2,1,0:T(8,128)S(1)} %bitcast.17), channel_id=1, replica_groups=mesh['xl'=2,'y'=8,'core'=2,'xh'=2,'z'=8] {'xl','y'}, dimensions={0} | all-to-all | bytes 524288 | tf_op jit(solution)/shard_map/all_to_all | solution.py:220
  76.6 1.9 %collective-permute-start.4 = (f32[32,128]{1,0:T(8,128)S(1)}, f32[32,128]{1,0:T(8,128)S(1)}, u32[]{:S(2)}, u32[]{:S(2)}) collective-permute-start(f32[32,128]{1,0:T(8,128)S(1)} %reduce_sum.19), channel_id=1, source_target_pairs={{0,20},{1,52},{2,84},{3,116},{4,148},{5,180},{6,212},{7,244},{8,26... | collective-permute-start | bytes 49160 | tf_op jit(solution)/shard_map/ppermute | solution.py:248
  78.6 7.0 %collective-permute-done.4 = f32[32,128]{1,0:T(8,128)S(1)} collective-permute-done((f32[32,128]{1,0:T(8,128)S(1)}, f32[32,128]{1,0:T(8,128)S(1)}, u32[]{:S(2)}, u32[]{:S(2)}) %collective-permute-start.4) | collective-permute-done | bytes 16416 | tf_op jit(solution)/shard_map/ppermute | solution.py:248
  85.6 16.0 %all_to_all.23 = f32[16,32,128]{2,1,0:T(8,128)S(1)} all-to-all(f32[16,32,128]{2,1,0:T(8,128)S(1)} %broadcast_in_dim.8), channel_id=1, replica_groups=mesh['xl'=2,'y'=8,'core'=2,'xh'=2,'z'=8] {'xh','z'}, dimensions={0} | all-to-all | bytes 524288 | tf_op jit(solution)/shard_map/all_to_all | solution.py:224
  101.6 0.7 reverse_select_fusion
  (9 shorter events, 0.1 us)
Async XLA Ops:
  1.8 3.5 %collective-permute-start = (f32[544,128]{1,0:T(8,128)S(1)}, f32[544,128]{1,0:T(8,128)S(1)}, u32[]{:S(2)}, u32[]{:S(2)}) collective-permute-start(f32[544,128]{1,0:T(8,128)S(1)} %get-tuple-element.27), channel_id=1, source_target_pairs={{0,16},{16,0},{1,17},{17,1},{2,18},{18,2},{3,19},{19,3},{4,20},{20... | collective-permute-start | bytes 835592 | tf_op jit(solution)/shard_map/ppermute | solution.py:217
  24.3 16.0 %collective-permute-start.1 = (f32[512,128]{1,0:T(8,128)S(1)}, f32[512,128]{1,0:T(8,128)S(1)}, u32[]{:S(2)}, u32[]{:S(2)}) collective-permute-start(f32[512,128]{1,0:T(8,128)S(1)} %get-tuple-element.28.green_ref), channel_id=1, source_target_pairs={{0,16},{16,0},{1,17},{17,1},{2,18},{18,2},{3,19},{19,3},{4,20},{20... | collective-permute-start | bytes 786440 | tf_op jit(solution)/shard_map/ppermute | solution.py:217
  26.3 14.1 %collective-permute-start.2 = (f32[512,128]{1,0:T(8,128)S(1)}, f32[512,128]{1,0:T(8,128)S(1)}, u32[]{:S(2)}, u32[]{:S(2)}) collective-permute-start(f32[512,128]{1,0:T(8,128)S(1)} %get-tuple-element.29.field_ref), channel_id=1, source_target_pairs={{0,16},{16,0},{1,17},{17,1},{2,18},{18,2},{3,19},{19,3},{4,20},{20... | collective-permute-start | bytes 786440 | tf_op jit(solution)/shard_map/ppermute | solution.py:217
  28.7 11.6 %collective-permute-start.3 = (f32[32,128]{1,0:T(8,128)S(1)}, f32[32,128]{1,0:T(8,128)S(1)}, u32[]{:S(2)}, u32[]{:S(2)}) collective-permute-start(f32[32,128]{1,0:T(8,128)S(1)} %reduce_sum.18), channel_id=1, source_target_pairs={{0,4},{1,36},{2,68},{3,100},{4,132},{5,164},{6,196},{7,228},{8,260... | collective-permute-start | bytes 49160 | tf_op jit(solution)/shard_map/ppermute | solution.py:241
  76.6 9.0 %collective-permute-start.4 = (f32[32,128]{1,0:T(8,128)S(1)}, f32[32,128]{1,0:T(8,128)S(1)}, u32[]{:S(2)}, u32[]{:S(2)}) collective-permute-start(f32[32,128]{1,0:T(8,128)S(1)} %reduce_sum.19), channel_id=1, source_target_pairs={{0,20},{1,52},{2,84},{3,116},{4,148},{5,180},{6,212},{7,244},{8,26... | collective-permute-start | bytes 49160 | tf_op jit(solution)/shard_map/ppermute | solution.py:248

commit v3 on v2

--- a/solution.py
+++ b/solution.py
@@ -47,18 +47,21 @@
     )
 
 
-def history(refs, part):
-    depth = refs[0].shape[0] // 4
+def history(refs, part, block):
+    depth = block // 4
     halves = [
-        jnp.concatenate([ref[pl.ds(2 * half + part, depth, stride=4), :] for ref in refs], axis=0)
+        jnp.concatenate([
+            ref[pl.ds(ref.shape[0] - last * block + 2 * half + part, depth, stride=4), :]
+            for ref in refs for last in (2, 1)
+        ], axis=0)
         for half in range(2)
     ]
     return jnp.concatenate(halves, axis=1)
 
 
-def image_of(left_re, left_im, refs):
+def image_of(left_re, left_im, refs, block):
     (re_high, re_low), (im_high, im_low) = split(left_re), split(left_im)
-    right_re, right_im = split(history(refs, 0)), split(history(refs, 1))
+    right_re, right_im = split(history(refs, 0, block)), split(history(refs, 1, block))
 
     def one(re_first, im_first, first, second):
         left = jnp.concatenate(
@@ -80,7 +83,7 @@
                 front * orbits:(front + 1) * orbits, half * lanes:(half + 1) * lanes]
 
 
-def half_image(init_ref, green_ref, field_ref, orbits, lower):
+def half_image(init_ref, sent_ref, orbits, lower, block):
     pairs = init_ref.shape[0] // 4
     re, im = (
         jnp.where(lower, init_ref[pl.ds(part, pairs, stride=2), :],
@@ -90,15 +93,20 @@
     sigma_re, sigma_im = sigma_pair(re, im, orbits)
     return image_of(
         jnp.concatenate([sigma_re, re], axis=1), jnp.concatenate([sigma_im, im], axis=1),
-        (green_ref, field_ref))
+        (sent_ref,), block)
 
 
 def first_kernel(orbits, order, init_ref, green_ref, field_ref,
-                 other_ref, near_ref, last_ref, flag_ref, init, green, field, sems):
+                 sent_ref, near_ref, last_ref, flag_ref, init, sems):
+    block = green_ref.shape[0]
+    end = sent_ref.shape[0]
     copies = [
         pltpu.make_async_copy(source, target, sems.at[n])
-        for n, (source, target) in enumerate(
-            ((init_ref, init), (green_ref, green), (field_ref, field)))
+        for n, (source, target) in enumerate((
+            (init_ref, init),
+            (green_ref, sent_ref.at[pl.ds(end - 2 * block, block)]),
+            (field_ref, sent_ref.at[pl.ds(end - block, block)]),
+        ))
     ]
     for copy in copies:
         copy.start()
@@ -115,18 +123,18 @@
         copy.wait()
     near_ref[...] = front(core * fronts + z)
     last_ref[...] = front((core + 1 + xh + xl) % 2 * fronts + z)
-    other_ref[rows:, :] = front((1 - core) * fronts + z)
-    for part, image in enumerate(half_image(init, green, field, orbits, core == 1)):
-        put(other_ref, part, image, orbits, order)
-
-
-def kept_kernel(orbits, order, init_ref, green_ref, field_ref, own_ref):
+    sent_ref[rows:rows + piece, :] = front((1 - core) * fronts + z)
+    for part, image in enumerate(half_image(init, sent_ref, orbits, core == 1, block)):
+        put(sent_ref, part, image, orbits, order)
+
+
+def kept_kernel(orbits, order, block, init_ref, sent_ref, own_ref):
     core = lax.axis_index("core")
-    for part, image in enumerate(half_image(init_ref, green_ref, field_ref, orbits, core == 0)):
+    for part, image in enumerate(half_image(init_ref, sent_ref, orbits, core == 0, block)):
         put(own_ref, part, image, orbits, order)
 
 
-def second_kernel(orbits, order, front_ref, green_ref, field_ref, green_far, field_far, out_ref):
+def second_kernel(orbits, order, block, front_ref, sent_ref, got_ref, out_ref):
     core = lax.axis_index("core")
     half_rows = front_ref.shape[0] // 2
 
@@ -144,7 +152,7 @@
         left_im += [sigma_im, im]
     images = image_of(
         jnp.concatenate(left_re, axis=1), jnp.concatenate(left_im, axis=1),
-        (green_ref, field_ref, green_far, field_far))
+        (sent_ref, got_ref), block)
     lanes = out_ref.shape[1]
     straight = (core + 1 + lax.axis_index("xh")) % 2 == 0
     for part, image in enumerate(images):
@@ -164,35 +172,34 @@
         functools.partial(first_kernel, orbits, order),
         out_shape=[
             jax.ShapeDtypeStruct((n, width), kind) for n, kind in (
-                (rows + 2 * orbits, jnp.float32), (2 * orbits, jnp.float32),
-                (2 * orbits, jnp.float32), (8, jnp.int32), (rows, jnp.float32),
-                (rows, jnp.float32), (rows, jnp.float32))
+                (rows + 2 * orbits + 2 * green.shape[0], jnp.float32), (2 * orbits, jnp.float32),
+                (2 * orbits, jnp.float32), (8, jnp.int32), (rows, jnp.float32))
         ],
         in_specs=[pl.BlockSpec(memory_space=pltpu.HBM)] * 3,
-        out_specs=[VMEM] * 7,
+        out_specs=[VMEM] * 5,
         scratch_shapes=[pltpu.SemaphoreType.DMA((3,))],
         compiler_params=LIMIT,
         name="first_collide",
     )(*operands)
 
 
-def kept_collide(init, green, field, orbits, order):
+def kept_collide(init, sent, orbits, order, block):
     return pl.pallas_call(
-        functools.partial(kept_kernel, orbits, order),
+        functools.partial(kept_kernel, orbits, order, block),
         out_shape=jax.ShapeDtypeStruct(init.shape, jnp.float32),
-        in_specs=[VMEM] * 3,
+        in_specs=[VMEM] * 2,
         out_specs=VMEM,
         compiler_params=LIMIT,
         cost_estimate=pl.CostEstimate(flops=10**8, bytes_accessed=10**6, transcendentals=0),
         name="kept_collide",
-    )(init, green, field)
-
-
-def second_collide(front, histories, orbits, order):
+    )(init, sent)
+
+
+def second_collide(front, histories, orbits, order, block):
     return pl.pallas_call(
-        functools.partial(second_kernel, orbits, order),
+        functools.partial(second_kernel, orbits, order, block),
         out_shape=jax.ShapeDtypeStruct(front.shape, jnp.float32),
-        in_specs=[VMEM] * 5,
+        in_specs=[VMEM] * 3,
         out_specs=VMEM,
         compiler_params=LIMIT,
         name="second_collide",
@@ -229,22 +236,17 @@
 
     green, field = tiles(green_hist), tiles(field_hist)
     order = [(y + zs // 2) % zs for y in range(ys)]
-    other, near, last, flag, init, green, field = first_collide(
-        init, green, field, orbits, order)
-    arrived = swap(other)
-    own = kept_collide(init, green, field, orbits, order)
+    block = green.shape[0]
+    sent, near, last, flag, init = first_collide(init, green, field, orbits, order)
+    got = swap(sent)
+    own = kept_collide(init, sent, orbits, order, block)
     flag = jnp.broadcast_to(flag == 0, (2, rows // 16, 8, width))
     own, flag = lax.optimization_barrier((own, flag))
-    piece = reduced(own + arrived[:rows])
-    near = jnp.where(lax.axis_index("xh") == lax.axis_index("core"), near, arrived[rows:])
-    green_late, field_late, piece = lax.optimization_barrier((green, field, piece))
-    turned = lax.ppermute(piece, EVERY, turns[0])
-    green_far = swap(green_late)
-    field_far = swap(field_late)
-    copies = copies_of(near, turned)
-    green_far, field_far, copies = lax.optimization_barrier((green_far, field_far, copies))
-    current = gathered(copies)
-    image = second_collide(current, (green, field, green_far, field_far), orbits, order)
+    piece = reduced(own + got[:rows])
+    near = jnp.where(
+        lax.axis_index("xh") == lax.axis_index("core"), near, got[rows:rows + 2 * orbits])
+    current = gathered(copies_of(near, lax.ppermute(piece, EVERY, turns[0])))
+    image = second_collide(current, (sent, got), orbits, order, block)
     turned = lax.ppermute(reduced(image), EVERY, turns[1])
     final = gathered(copies_of(last, turned)).reshape(2, -1, 8, width)
     return jnp.where(flag, final, final[::-1]).reshape(front_init.shape)

time: 103 us -> 98.6 us (0.957)
  starting transfers between devices: 18.4 us -> 14.1 us
    ppermute x3 -> x1, starting transfers between devices: 6.25 us -> 1.92 us  [swap(): return lax.ppermute(value, 'core', [(0, 1), (1, 0)])]
  transfers between devices with their start and end apart: 5 -> 3, of which waited for: 3 -> 3; matrix products, arithmetic and copies ran while one was open for 0% -> 0% of each run, Pallas kernels for 1% -> 1%
where the time goes in v3:
time: 98.6 us; the launch traced here: 98.3 us
  blocking collectives  69.7 us (71%)
  starting transfers between devices  14.1 us (14%)
  waiting for transfers between devices  9.98 us (10%)
  Pallas kernels  3.64 us (4%)
    all_to_all x2, blocking collectives, gathered(): return lax.all_to_all(copies, B, 0, 0, tiled=True).reshape(rows, width)  37.1 us
    all_to_all x2, blocking collectives, reduced(): lax.all_to_all(partial_sum.reshape(fronts, -1, width), A, 0, 0, tiled=True)  32.6 us
    ppermute x1, starting transfers between devices, corrector(): current = gathered(copies_of(near, lax.ppermute(piece, EVERY, turns[0])))  10.2 us
    ppermute x1, waiting for transfers between devices, corrector(): turned = lax.ppermute(reduced(image), EVERY, turns[1])  7.04 us
  transfers between devices with their start and end apart: 3, of which 3 were waited for; matrix products, arithmetic and copies ran while one was open for 0% of the time, Pallas kernels for 1%

profile of v3, /device:TPU:8, one launch (start us, length us, event | category | flops | bytes accessed | tf_op | source)
XLA Modules:
  0.0 98.3 jit_solution(2208457781009490958)
XLA Ops:
  0.0 1.8 %first_collide.1 = (f32[1568,128]{1,0:T(8,128)S(1)}, f32[32,128]{1,0:T(8,128)S(1)}, f32[32,128]{1,0:T(8,128)S(1)}, s32[8,128]{1,0:T(8,128)S(1)}, f32[512,128]{1,0:T(8,128)S(1)}) custom-call(f32[512,128]{1,0:T(8,128)} %bitcast.20, f32[512,128]{1,0:T(8,128)} %bitcast.21, f32[512,128]{1,0:T(8,128)} %bitcast.22), custom_call_target="tpu_custom_call" | custom-call | tf_op jit(solution)/shard_map/first_collide/pallas_call | solution.py:171
  1.8 1.9 %collective-permute-start = (f32[1568,128]{1,0:T(8,128)S(1)}, f32[1568,128]{1,0:T(8,128)S(1)}, u32[]{:S(2)}, u32[]{:S(2)}) collective-permute-start(f32[1568,128]{1,0:T(8,128)S(1)} %get-tuple-element.13.sent_ref), channel_id=1, source_target_pairs={{0,16},{16,0},{1,17},{17,1},{2,18},{18,2},{3,19},{19,3},{4,20},{20... | collective-permute-start | bytes 2408456 | tf_op jit(solution)/shard_map/ppermute | solution.py:224
  3.8 0.7 kept_collide.1
  4.5 1.5 %collective-permute-done.got_ref = f32[1568,128]{1,0:T(8,128)S(1)} collective-permute-done((f32[1568,128]{1,0:T(8,128)S(1)}, f32[1568,128]{1,0:T(8,128)S(1)}, u32[]{:S(2)}, u32[]{:S(2)}) %collective-permute-start) | collective-permute-done | bytes 802848 | tf_op jit(solution)/shard_map/ppermute | solution.py:224
  6.1 19.0 %all_to_all.20 = f32[16,32,128]{2,1,0:T(8,128)S(1)} all-to-all(f32[16,32,128]{2,1,0:T(8,128)S(1)} %bitcast.18), channel_id=1, replica_groups=mesh['xl'=2,'y'=8,'core'=2,'xh'=2,'z'=8] {'xl','y'}, dimensions={0} | all-to-all | bytes 524288 | tf_op jit(solution)/shard_map/all_to_all | solution.py:227
  25.1 10.2 %collective-permute-start.1 = (f32[32,128]{1,0:T(8,128)S(1)}, f32[32,128]{1,0:T(8,128)S(1)}, u32[]{:S(2)}, u32[]{:S(2)}) collective-permute-start(f32[32,128]{1,0:T(8,128)S(1)} %reduce_sum.18), channel_id=1, source_target_pairs={{0,4},{1,36},{2,68},{3,100},{4,132},{5,164},{6,196},{7,228},{8,260... | collective-permute-start | bytes 49160 | tf_op jit(solution)/shard_map/ppermute | solution.py:248
  35.3 1.4 %collective-permute-done.1 = f32[32,128]{1,0:T(8,128)S(1)} collective-permute-done((f32[32,128]{1,0:T(8,128)S(1)}, f32[32,128]{1,0:T(8,128)S(1)}, u32[]{:S(2)}, u32[]{:S(2)}) %collective-permute-start.1) | collective-permute-done | bytes 16416 | tf_op jit(solution)/shard_map/ppermute | solution.py:248
  36.8 21.4 %all_to_all.21 = f32[16,32,128]{2,1,0:T(8,128)S(1)} all-to-all(f32[16,32,128]{2,1,0:T(8,128)S(1)} %broadcast_in_dim.7), channel_id=1, replica_groups=mesh['xl'=2,'y'=8,'core'=2,'xh'=2,'z'=8] {'xh','z'}, dimensions={0} | all-to-all | bytes 524288 | tf_op jit(solution)/shard_map/all_to_all | solution.py:231
  58.1 1.1 %second_collide.1 = f32[512,128]{1,0:T(8,128)S(1)} custom-call(f32[512,128]{1,0:T(8,128)S(1)} %bitcast.16, f32[1568,128]{1,0:T(8,128)S(1)} %get-tuple-element.13.sent_ref, f32[1568,128]{1,0:T(8,128)S(1)} %collective-permute-done.got_ref), custom_call_target="tpu_custom_call" | custom-call | tf_op jit(solution)/shard_map/second_collide/pallas_call | solution.py:199
  59.2 13.6 %all_to_all.22 = f32[16,32,128]{2,1,0:T(8,128)S(1)} all-to-all(f32[16,32,128]{2,1,0:T(8,128)S(1)} %bitcast.17), channel_id=1, replica_groups=mesh['xl'=2,'y'=8,'core'=2,'xh'=2,'z'=8] {'xl','y'}, dimensions={0} | all-to-all | bytes 524288 | tf_op jit(solution)/shard_map/all_to_all | solution.py:227
  72.8 1.9 %collective-permute-start.2 = (f32[32,128]{1,0:T(8,128)S(1)}, f32[32,128]{1,0:T(8,128)S(1)}, u32[]{:S(2)}, u32[]{:S(2)}) collective-permute-start(f32[32,128]{1,0:T(8,128)S(1)} %reduce_sum.19), channel_id=1, source_target_pairs={{0,20},{1,52},{2,84},{3,116},{4,148},{5,180},{6,212},{7,244},{8,26... | collective-permute-start | bytes 49160 | tf_op jit(solution)/shard_map/ppermute | solution.py:250
  74.8 7.0 %collective-permute-done.2 = f32[32,128]{1,0:T(8,128)S(1)} collective-permute-done((f32[32,128]{1,0:T(8,128)S(1)}, f32[32,128]{1,0:T(8,128)S(1)}, u32[]{:S(2)}, u32[]{:S(2)}) %collective-permute-start.2) | collective-permute-done | bytes 16416 | tf_op jit(solution)/shard_map/ppermute | solution.py:250
  81.8 15.7 %all_to_all.23 = f32[16,32,128]{2,1,0:T(8,128)S(1)} all-to-all(f32[16,32,128]{2,1,0:T(8,128)S(1)} %broadcast_in_dim.8), channel_id=1, replica_groups=mesh['xl'=2,'y'=8,'core'=2,'xh'=2,'z'=8] {'xh','z'}, dimensions={0} | all-to-all | bytes 524288 | tf_op jit(solution)/shard_map/all_to_all | solution.py:231
  97.6 0.7 reverse_select_fusion
  (9 shorter events, 0.1 us)
Async XLA Ops:
  1.8 4.2 %collective-permute-start = (f32[1568,128]{1,0:T(8,128)S(1)}, f32[1568,128]{1,0:T(8,128)S(1)}, u32[]{:S(2)}, u32[]{:S(2)}) collective-permute-start(f32[1568,128]{1,0:T(8,128)S(1)} %get-tuple-element.13.sent_ref), channel_id=1, source_target_pairs={{0,16},{16,0},{1,17},{17,1},{2,18},{18,2},{3,19},{19,3},{4,20},{20... | collective-permute-start | bytes 2408456 | tf_op jit(solution)/shard_map/ppermute | solution.py:224
  25.1 11.6 %collective-permute-start.1 = (f32[32,128]{1,0:T(8,128)S(1)}, f32[32,128]{1,0:T(8,128)S(1)}, u32[]{:S(2)}, u32[]{:S(2)}) collective-permute-start(f32[32,128]{1,0:T(8,128)S(1)} %reduce_sum.18), channel_id=1, source_target_pairs={{0,4},{1,36},{2,68},{3,100},{4,132},{5,164},{6,196},{7,228},{8,260... | collective-permute-start | bytes 49160 | tf_op jit(solution)/shard_map/ppermute | solution.py:248
  72.8 9.0 %collective-permute-start.2 = (f32[32,128]{1,0:T(8,128)S(1)}, f32[32,128]{1,0:T(8,128)S(1)}, u32[]{:S(2)}, u32[]{:S(2)}) collective-permute-start(f32[32,128]{1,0:T(8,128)S(1)} %reduce_sum.19), channel_id=1, source_target_pairs={{0,20},{1,52},{2,84},{3,116},{4,148},{5,180},{6,212},{7,244},{8,26... | collective-permute-start | bytes 49160 | tf_op jit(solution)/shard_map/ppermute | solution.py:250

commit v4 on v3

--- a/solution.py
+++ b/solution.py
@@ -83,55 +83,53 @@
                 front * orbits:(front + 1) * orbits, half * lanes:(half + 1) * lanes]
 
 
-def half_image(init_ref, sent_ref, orbits, lower, block):
-    pairs = init_ref.shape[0] // 4
-    re, im = (
-        jnp.where(lower, init_ref[pl.ds(part, pairs, stride=2), :],
-                  init_ref[pl.ds(2 * pairs + part, pairs, stride=2), :])
-        for part in range(2)
-    )
+def half_image(front_ref, buffer_ref, orbits, block):
+    pairs = orbits * orbits // 2
+    re, im = (front_ref[pl.ds(part, pairs, stride=2), :] for part in range(2))
     sigma_re, sigma_im = sigma_pair(re, im, orbits)
     return image_of(
         jnp.concatenate([sigma_re, re], axis=1), jnp.concatenate([sigma_im, im], axis=1),
-        (sent_ref,), block)
-
-
-def first_kernel(orbits, order, init_ref, green_ref, field_ref,
-                 sent_ref, near_ref, last_ref, flag_ref, init, sems):
-    block = green_ref.shape[0]
-    end = sent_ref.shape[0]
+        (buffer_ref,), block)
+
+
+def load_kernel(fronts, init_ref, green_ref, field_ref,
+                sent_ref, mine_ref, last_ref, flag_ref, sems):
+    core, xl, xh, z = (lax.axis_index(axis) for axis in ("core", "xl", "xh", "z"))
+    half, piece, block = mine_ref.shape[0], last_ref.shape[0], green_ref.shape[0]
+
+    def rows_of(index, count):
+        return init_ref.at[pl.ds(pl.multiple_of(index * count, count), count)]
+
     copies = [
         pltpu.make_async_copy(source, target, sems.at[n])
         for n, (source, target) in enumerate((
-            (init_ref, init),
-            (green_ref, sent_ref.at[pl.ds(end - 2 * block, block)]),
-            (field_ref, sent_ref.at[pl.ds(end - block, block)]),
+            (rows_of(1 - core, half), sent_ref.at[pl.ds(0, half)]),
+            (green_ref, sent_ref.at[pl.ds(half, block)]),
+            (field_ref, sent_ref.at[pl.ds(half + block, block)]),
+            (rows_of(core, half), mine_ref),
+            (rows_of((core + 1 + xh + xl) % 2 * fronts + z, piece), last_ref),
         ))
     ]
     for copy in copies:
         copy.start()
-    core, xl, xh, z = (lax.axis_index(axis) for axis in ("core", "xl", "xh", "z"))
-    fronts = len(order)
-    piece = 2 * orbits
-    rows = init.shape[0]
     flag_ref[...] = jnp.full(flag_ref.shape, (core + 1 + xl) % 2, jnp.int32)
-
-    def front(index):
-        return init[pl.ds(pl.multiple_of(index * piece, piece), piece), :]
-
     for copy in copies:
         copy.wait()
-    near_ref[...] = front(core * fronts + z)
-    last_ref[...] = front((core + 1 + xh + xl) % 2 * fronts + z)
-    sent_ref[rows:rows + piece, :] = front((1 - core) * fronts + z)
-    for part, image in enumerate(half_image(init, sent_ref, orbits, core == 1, block)):
-        put(sent_ref, part, image, orbits, order)
-
-
-def kept_kernel(orbits, order, block, init_ref, sent_ref, own_ref):
-    core = lax.axis_index("core")
-    for part, image in enumerate(half_image(init_ref, sent_ref, orbits, core == 0, block)):
+
+
+def near_kernel(orbits, order, block, mine_ref, sent_ref, own_ref):
+    for part, image in enumerate(half_image(mine_ref, sent_ref, orbits, block)):
         put(own_ref, part, image, orbits, order)
+
+
+def far_kernel(orbits, order, block, mine_ref, own_ref, got_ref, chip_ref, piece_ref):
+    core, xh, z = (lax.axis_index(axis) for axis in ("core", "xh", "z"))
+    piece = piece_ref.shape[0]
+    here = pl.ds(pl.multiple_of(z * piece, piece), piece)
+    piece_ref[...] = jnp.where(xh == core, mine_ref[here, :], got_ref[here, :])
+    for part, image in enumerate(half_image(got_ref, got_ref, orbits, block)):
+        put(chip_ref, part, image, orbits, order)
+    chip_ref[...] += own_ref[...]
 
 
 def second_kernel(orbits, order, block, front_ref, sent_ref, got_ref, out_ref):
@@ -165,34 +163,49 @@
 LIMIT = pltpu.CompilerParams(vmem_limit_bytes=12 << 20)
 
 
-def first_collide(init, green, field, orbits, order):
+def load(init, green, field, fronts):
     rows, width = init.shape
     operands = [pltpu.with_memory_space_constraint(x, pltpu.HBM) for x in (init, green, field)]
     return pl.pallas_call(
-        functools.partial(first_kernel, orbits, order),
+        functools.partial(load_kernel, fronts // 2),
         out_shape=[
             jax.ShapeDtypeStruct((n, width), kind) for n, kind in (
-                (rows + 2 * orbits + 2 * green.shape[0], jnp.float32), (2 * orbits, jnp.float32),
-                (2 * orbits, jnp.float32), (8, jnp.int32), (rows, jnp.float32))
+                (rows // 2 + 2 * green.shape[0], jnp.float32), (rows // 2, jnp.float32),
+                (rows // fronts, jnp.float32), (8, jnp.int32))
         ],
         in_specs=[pl.BlockSpec(memory_space=pltpu.HBM)] * 3,
-        out_specs=[VMEM] * 5,
-        scratch_shapes=[pltpu.SemaphoreType.DMA((3,))],
-        compiler_params=LIMIT,
-        name="first_collide",
+        out_specs=[VMEM] * 4,
+        scratch_shapes=[pltpu.SemaphoreType.DMA((5,))],
+        compiler_params=LIMIT,
+        name="load",
     )(*operands)
 
 
-def kept_collide(init, sent, orbits, order, block):
-    return pl.pallas_call(
-        functools.partial(kept_kernel, orbits, order, block),
-        out_shape=jax.ShapeDtypeStruct(init.shape, jnp.float32),
+def near_collide(mine, sent, orbits, order, block):
+    rows, width = mine.shape
+    return pl.pallas_call(
+        functools.partial(near_kernel, orbits, order, block),
+        out_shape=jax.ShapeDtypeStruct((2 * rows, width), jnp.float32),
         in_specs=[VMEM] * 2,
         out_specs=VMEM,
         compiler_params=LIMIT,
         cost_estimate=pl.CostEstimate(flops=10**8, bytes_accessed=10**6, transcendentals=0),
-        name="kept_collide",
-    )(init, sent)
+        name="near_collide",
+    )(mine, sent)
+
+
+def far_collide(mine, own, got, orbits, order, block):
+    return pl.pallas_call(
+        functools.partial(far_kernel, orbits, order, block),
+        out_shape=[
+            jax.ShapeDtypeStruct((n, own.shape[1]), jnp.float32)
+            for n in (own.shape[0], 2 * orbits)
+        ],
+        in_specs=[VMEM] * 3,
+        out_specs=[VMEM] * 2,
+        compiler_params=LIMIT,
+        name="far_collide",
+    )(mine, own, got)
 
 
 def second_collide(front, histories, orbits, order, block):
@@ -237,15 +250,13 @@
     green, field = tiles(green_hist), tiles(field_hist)
     order = [(y + zs // 2) % zs for y in range(ys)]
     block = green.shape[0]
-    sent, near, last, flag, init = first_collide(init, green, field, orbits, order)
+    sent, mine, last, flag = load(init, green, field, fronts)
     got = swap(sent)
-    own = kept_collide(init, sent, orbits, order, block)
+    own = near_collide(mine, sent, orbits, order, block)
     flag = jnp.broadcast_to(flag == 0, (2, rows // 16, 8, width))
     own, flag = lax.optimization_barrier((own, flag))
-    piece = reduced(own + got[:rows])
-    near = jnp.where(
-        lax.axis_index("xh") == lax.axis_index("core"), near, got[rows:rows + 2 * orbits])
-    current = gathered(copies_of(near, lax.ppermute(piece, EVERY, turns[0])))
+    chip, near = far_collide(mine, own, got, orbits, order, block)
+    current = gathered(copies_of(near, lax.ppermute(reduced(chip), EVERY, turns[0])))
     image = second_collide(current, (sent, got), orbits, order, block)
     turned = lax.ppermute(reduced(image), EVERY, turns[1])
     final = gathered(copies_of(last, turned)).reshape(2, -1, 8, width)

time: 98.6 us -> 98.4 us (level)
    pallas_call x2 -> x3, Pallas kernels: 2.54 us -> 2.58 us  [the longest x1 1.17 us: load(): pl.pallas_call(functools.partial(load_kernel, fronts // 2), out_shape=[ja...]
where the time goes in v4:
time: 98.4 us; the launch traced here: 98.1 us
  blocking collectives  69.6 us (71%)
  starting transfers between devices  14.1 us (14%)
  waiting for transfers between devices  9.78 us (10%)
  Pallas kernels  3.68 us (4%)
    all_to_all x2, blocking collectives, gathered(): return lax.all_to_all(copies, B, 0, 0, tiled=True).reshape(rows, width)  37.1 us
    all_to_all x2, blocking collectives, reduced(): lax.all_to_all(partial_sum.reshape(fronts, -1, width), A, 0, 0, tiled=True)  32.6 us
    ppermute x1, starting transfers between devices, corrector(): lax.ppermute(reduced(chip), EVERY, turns[0])  10.2 us
    ppermute x1, waiting for transfers between devices, corrector(): turned = lax.ppermute(reduced(image), EVERY, turns[1])  7.04 us
  transfers between devices with their start and end apart: 3, of which 3 were waited for; matrix products, arithmetic and copies ran while one was open for 0% of the time, Pallas kernels for 1%

profile of v4, /device:TPU:8, one launch (start us, length us, event | category | flops | bytes accessed | tf_op | source)
XLA Modules:
  0.0 98.1 jit_solution(12004964594257122519)
XLA Ops:
  0.0 1.2 %load.1 = (f32[1280,128]{1,0:T(8,128)S(1)}, f32[256,128]{1,0:T(8,128)S(1)}, f32[32,128]{1,0:T(8,128)S(1)}, s32[8,128]{1,0:T(8,128)S(1)}) custom-call(f32[512,128]{1,0:T(8,128)} %bitcast.20, f32[512,128]{1,0:T(8,128)} %bitcast.21, f32[512,128]{1,0:T(8,128)} %bitcast.22), custom_call_target="tpu_custom_call" | custom-call | tf_op jit(solution)/shard_map/load/pallas_call | solution.py:169
  1.2 1.9 %collective-permute-start = (f32[1280,128]{1,0:T(8,128)S(1)}, f32[1280,128]{1,0:T(8,128)S(1)}, u32[]{:S(2)}, u32[]{:S(2)}) collective-permute-start(f32[1280,128]{1,0:T(8,128)S(1)} %get-tuple-element.14.sent_ref), channel_id=1, source_target_pairs={{0,16},{16,0},{1,17},{17,1},{2,18},{18,2},{3,19},{19,3},{4,20},{20... | collective-permute-start | bytes 1966088 | tf_op jit(solution)/shard_map/ppermute | solution.py:237
  3.1 0.7 near_collide.1.own_ref
  3.9 1.3 %collective-permute-done.got_ref = f32[1280,128]{1,0:T(8,128)S(1)} collective-permute-done((f32[1280,128]{1,0:T(8,128)S(1)}, f32[1280,128]{1,0:T(8,128)S(1)}, u32[]{:S(2)}, u32[]{:S(2)}) %collective-permute-start) | collective-permute-done | bytes 655392 | tf_op jit(solution)/shard_map/ppermute | solution.py:237
  5.2 0.7 far_collide.1
  5.9 19.0 %all_to_all.20 = f32[16,32,128]{2,1,0:T(8,128)S(1)} all-to-all(f32[16,32,128]{2,1,0:T(8,128)S(1)} %bitcast.18), channel_id=1, replica_groups=mesh['xl'=2,'y'=8,'core'=2,'xh'=2,'z'=8] {'xl','y'}, dimensions={0} | all-to-all | bytes 524288 | tf_op jit(solution)/shard_map/all_to_all | solution.py:240
  24.9 10.2 %collective-permute-start.1 = (f32[32,128]{1,0:T(8,128)S(1)}, f32[32,128]{1,0:T(8,128)S(1)}, u32[]{:S(2)}, u32[]{:S(2)}) collective-permute-start(f32[32,128]{1,0:T(8,128)S(1)} %reduce_sum.18), channel_id=1, source_target_pairs={{0,4},{1,36},{2,68},{3,100},{4,132},{5,164},{6,196},{7,228},{8,260... | collective-permute-start | bytes 49160 | tf_op jit(solution)/shard_map/ppermute | solution.py:259
  35.1 1.4 %collective-permute-done.1 = f32[32,128]{1,0:T(8,128)S(1)} collective-permute-done((f32[32,128]{1,0:T(8,128)S(1)}, f32[32,128]{1,0:T(8,128)S(1)}, u32[]{:S(2)}, u32[]{:S(2)}) %collective-permute-start.1) | collective-permute-done | bytes 16416 | tf_op jit(solution)/shard_map/ppermute | solution.py:259
  36.6 21.4 %all_to_all.21 = f32[16,32,128]{2,1,0:T(8,128)S(1)} all-to-all(f32[16,32,128]{2,1,0:T(8,128)S(1)} %broadcast_in_dim.7), channel_id=1, replica_groups=mesh['xl'=2,'y'=8,'core'=2,'xh'=2,'z'=8] {'xh','z'}, dimensions={0} | all-to-all | bytes 524288 | tf_op jit(solution)/shard_map/all_to_all | solution.py:244
  57.9 1.1 %second_collide.1 = f32[512,128]{1,0:T(8,128)S(1)} custom-call(f32[512,128]{1,0:T(8,128)S(1)} %bitcast.16, f32[1280,128]{1,0:T(8,128)S(1)} %get-tuple-element.14.sent_ref, f32[1280,128]{1,0:T(8,128)S(1)} %collective-permute-done.got_ref), custom_call_target="tpu_custom_call" | custom-call | tf_op jit(solution)/shard_map/second_collide/pallas_call | solution.py:212
  59.0 13.6 %all_to_all.22 = f32[16,32,128]{2,1,0:T(8,128)S(1)} all-to-all(f32[16,32,128]{2,1,0:T(8,128)S(1)} %bitcast.17), channel_id=1, replica_groups=mesh['xl'=2,'y'=8,'core'=2,'xh'=2,'z'=8] {'xl','y'}, dimensions={0} | all-to-all | bytes 524288 | tf_op jit(solution)/shard_map/all_to_all | solution.py:240
  72.7 1.9 %collective-permute-start.2 = (f32[32,128]{1,0:T(8,128)S(1)}, f32[32,128]{1,0:T(8,128)S(1)}, u32[]{:S(2)}, u32[]{:S(2)}) collective-permute-start(f32[32,128]{1,0:T(8,128)S(1)} %reduce_sum.19), channel_id=1, source_target_pairs={{0,20},{1,52},{2,84},{3,116},{4,148},{5,180},{6,212},{7,244},{8,26... | collective-permute-start | bytes 49160 | tf_op jit(solution)/shard_map/ppermute | solution.py:261
  74.6 7.0 %collective-permute-done.2 = f32[32,128]{1,0:T(8,128)S(1)} collective-permute-done((f32[32,128]{1,0:T(8,128)S(1)}, f32[32,128]{1,0:T(8,128)S(1)}, u32[]{:S(2)}, u32[]{:S(2)}) %collective-permute-start.2) | collective-permute-done | bytes 16416 | tf_op jit(solution)/shard_map/ppermute | solution.py:261
  81.7 15.7 %all_to_all.23 = f32[16,32,128]{2,1,0:T(8,128)S(1)} all-to-all(f32[16,32,128]{2,1,0:T(8,128)S(1)} %broadcast_in_dim.8), channel_id=1, replica_groups=mesh['xl'=2,'y'=8,'core'=2,'xh'=2,'z'=8] {'xh','z'}, dimensions={0} | all-to-all | bytes 524288 | tf_op jit(solution)/shard_map/all_to_all | solution.py:244
  97.4 0.7 reverse_select_fusion
  (8 shorter events, 0.1 us)
Async XLA Ops:
  1.2 4.0 %collective-permute-start = (f32[1280,128]{1,0:T(8,128)S(1)}, f32[1280,128]{1,0:T(8,128)S(1)}, u32[]{:S(2)}, u32[]{:S(2)}) collective-permute-start(f32[1280,128]{1,0:T(8,128)S(1)} %get-tuple-element.14.sent_ref), channel_id=1, source_target_pairs={{0,16},{16,0},{1,17},{17,1},{2,18},{18,2},{3,19},{19,3},{4,20},{20... | collective-permute-start | bytes 1966088 | tf_op jit(solution)/shard_map/ppermute | solution.py:237
  24.9 11.6 %collective-permute-start.1 = (f32[32,128]{1,0:T(8,128)S(1)}, f32[32,128]{1,0:T(8,128)S(1)}, u32[]{:S(2)}, u32[]{:S(2)}) collective-permute-start(f32[32,128]{1,0:T(8,128)S(1)} %reduce_sum.18), channel_id=1, source_target_pairs={{0,4},{1,36},{2,68},{3,100},{4,132},{5,164},{6,196},{7,228},{8,260... | collective-permute-start | bytes 49160 | tf_op jit(solution)/shard_map/ppermute | solution.py:259
  72.7 9.0 %collective-permute-start.2 = (f32[32,128]{1,0:T(8,128)S(1)}, f32[32,128]{1,0:T(8,128)S(1)}, u32[]{:S(2)}, u32[]{:S(2)}) collective-permute-start(f32[32,128]{1,0:T(8,128)S(1)} %reduce_sum.19), channel_id=1, source_target_pairs={{0,20},{1,52},{2,84},{3,116},{4,148},{5,180},{6,212},{7,244},{8,26... | collective-permute-start | bytes 49160 | tf_op jit(solution)/shard_map/ppermute | solution.py:261

commit v5 on v4

--- a/solution.py
+++ b/solution.py
@@ -74,13 +74,14 @@
     return one(re, (-im_high, -im_low), right_re, right_im), one(re, im, right_im, right_re)
 
 
-def put(target_ref, part, image, orbits, order):
+def put(target_ref, part, image, orbits, order, base_ref=None):
     lanes = target_ref.shape[1]
     for half in range(2):
         for place, front in enumerate(order):
             first = (half * len(order) + place) * 2 * orbits + part
-            target_ref[pl.ds(first, orbits, stride=2), :] = image[
-                front * orbits:(front + 1) * orbits, half * lanes:(half + 1) * lanes]
+            here = pl.ds(first, orbits, stride=2)
+            value = image[front * orbits:(front + 1) * orbits, half * lanes:(half + 1) * lanes]
+            target_ref[here, :] = value if base_ref is None else value + base_ref[here, :]
 
 
 def half_image(front_ref, buffer_ref, orbits, block):
@@ -128,8 +129,7 @@
     here = pl.ds(pl.multiple_of(z * piece, piece), piece)
     piece_ref[...] = jnp.where(xh == core, mine_ref[here, :], got_ref[here, :])
     for part, image in enumerate(half_image(got_ref, got_ref, orbits, block)):
-        put(chip_ref, part, image, orbits, order)
-    chip_ref[...] += own_ref[...]
+        put(chip_ref, part, image, orbits, order, own_ref)
 
 
 def second_kernel(orbits, order, block, front_ref, sent_ref, got_ref, out_ref):

time: 98.4 us -> 98.4 us (level)
  no operation moved by 1% of the time
where the time goes in v5:
time: 98.4 us; the launch traced here: 98.1 us
  blocking collectives  69.6 us (71%)
  starting transfers between devices  14.1 us (14%)
  waiting for transfers between devices  9.78 us (10%)
  Pallas kernels  3.66 us (4%)
    all_to_all x2, blocking collectives, gathered(): return lax.all_to_all(copies, B, 0, 0, tiled=True).reshape(rows, width)  37.1 us
    all_to_all x2, blocking collectives, reduced(): lax.all_to_all(partial_sum.reshape(fronts, -1, width), A, 0, 0, tiled=True)  32.6 us
    ppermute x1, starting transfers between devices, corrector(): lax.ppermute(reduced(chip), EVERY, turns[0])  10.2 us
    ppermute x1, waiting for transfers between devices, corrector(): turned = lax.ppermute(reduced(image), EVERY, turns[1])  7.04 us
  transfers between devices with their start and end apart: 3, of which 3 were waited for; matrix products, arithmetic and copies ran while one was open for 0% of the time, Pallas kernels for 1%

profile of v5, /device:TPU:8, one launch (start us, length us, event | category | flops | bytes accessed | tf_op | source)
XLA Modules:
  0.0 98.1 jit_solution(1670957790199288556)
XLA Ops:
  0.0 1.2 %load.1 = (f32[1280,128]{1,0:T(8,128)S(1)}, f32[256,128]{1,0:T(8,128)S(1)}, f32[32,128]{1,0:T(8,128)S(1)}, s32[8,128]{1,0:T(8,128)S(1)}) custom-call(f32[512,128]{1,0:T(8,128)} %bitcast.20, f32[512,128]{1,0:T(8,128)} %bitcast.21, f32[512,128]{1,0:T(8,128)} %bitcast.22), custom_call_target="tpu_custom_call" | custom-call | tf_op jit(solution)/shard_map/load/pallas_call | solution.py:169
  1.2 1.9 %collective-permute-start = (f32[1280,128]{1,0:T(8,128)S(1)}, f32[1280,128]{1,0:T(8,128)S(1)}, u32[]{:S(2)}, u32[]{:S(2)}) collective-permute-start(f32[1280,128]{1,0:T(8,128)S(1)} %get-tuple-element.14.sent_ref), channel_id=1, source_target_pairs={{0,16},{16,0},{1,17},{17,1},{2,18},{18,2},{3,19},{19,3},{4,20},{20... | collective-permute-start | bytes 1966088 | tf_op jit(solution)/shard_map/ppermute | solution.py:237
  3.1 0.7 near_collide.1.own_ref
  3.9 1.3 %collective-permute-done.got_ref = f32[1280,128]{1,0:T(8,128)S(1)} collective-permute-done((f32[1280,128]{1,0:T(8,128)S(1)}, f32[1280,128]{1,0:T(8,128)S(1)}, u32[]{:S(2)}, u32[]{:S(2)}) %collective-permute-start) | collective-permute-done | bytes 655392 | tf_op jit(solution)/shard_map/ppermute | solution.py:237
  5.2 0.7 far_collide.1
  5.9 19.0 %all_to_all.20 = f32[16,32,128]{2,1,0:T(8,128)S(1)} all-to-all(f32[16,32,128]{2,1,0:T(8,128)S(1)} %bitcast.18), channel_id=1, replica_groups=mesh['xl'=2,'y'=8,'core'=2,'xh'=2,'z'=8] {'xl','y'}, dimensions={0} | all-to-all | bytes 524288 | tf_op jit(solution)/shard_map/all_to_all | solution.py:240
  24.9 10.2 %collective-permute-start.1 = (f32[32,128]{1,0:T(8,128)S(1)}, f32[32,128]{1,0:T(8,128)S(1)}, u32[]{:S(2)}, u32[]{:S(2)}) collective-permute-start(f32[32,128]{1,0:T(8,128)S(1)} %reduce_sum.18), channel_id=1, source_target_pairs={{0,4},{1,36},{2,68},{3,100},{4,132},{5,164},{6,196},{7,228},{8,260... | collective-permute-start | bytes 49160 | tf_op jit(solution)/shard_map/ppermute | solution.py:259
  35.1 1.4 %collective-permute-done.1 = f32[32,128]{1,0:T(8,128)S(1)} collective-permute-done((f32[32,128]{1,0:T(8,128)S(1)}, f32[32,128]{1,0:T(8,128)S(1)}, u32[]{:S(2)}, u32[]{:S(2)}) %collective-permute-start.1) | collective-permute-done | bytes 16416 | tf_op jit(solution)/shard_map/ppermute | solution.py:259
  36.6 21.4 %all_to_all.21 = f32[16,32,128]{2,1,0:T(8,128)S(1)} all-to-all(f32[16,32,128]{2,1,0:T(8,128)S(1)} %broadcast_in_dim.7), channel_id=1, replica_groups=mesh['xl'=2,'y'=8,'core'=2,'xh'=2,'z'=8] {'xh','z'}, dimensions={0} | all-to-all | bytes 524288 | tf_op jit(solution)/shard_map/all_to_all | solution.py:244
  57.9 1.1 %second_collide.1 = f32[512,128]{1,0:T(8,128)S(1)} custom-call(f32[512,128]{1,0:T(8,128)S(1)} %bitcast.16, f32[1280,128]{1,0:T(8,128)S(1)} %get-tuple-element.14.sent_ref, f32[1280,128]{1,0:T(8,128)S(1)} %collective-permute-done.got_ref), custom_call_target="tpu_custom_call" | custom-call | tf_op jit(solution)/shard_map/second_collide/pallas_call | solution.py:212
  59.0 13.6 %all_to_all.22 = f32[16,32,128]{2,1,0:T(8,128)S(1)} all-to-all(f32[16,32,128]{2,1,0:T(8,128)S(1)} %bitcast.17), channel_id=1, replica_groups=mesh['xl'=2,'y'=8,'core'=2,'xh'=2,'z'=8] {'xl','y'}, dimensions={0} | all-to-all | bytes 524288 | tf_op jit(solution)/shard_map/all_to_all | solution.py:240
  72.6 1.9 %collective-permute-start.2 = (f32[32,128]{1,0:T(8,128)S(1)}, f32[32,128]{1,0:T(8,128)S(1)}, u32[]{:S(2)}, u32[]{:S(2)}) collective-permute-start(f32[32,128]{1,0:T(8,128)S(1)} %reduce_sum.19), channel_id=1, source_target_pairs={{0,20},{1,52},{2,84},{3,116},{4,148},{5,180},{6,212},{7,244},{8,26... | collective-permute-start | bytes 49160 | tf_op jit(solution)/shard_map/ppermute | solution.py:261
  74.6 7.0 %collective-permute-done.2 = f32[32,128]{1,0:T(8,128)S(1)} collective-permute-done((f32[32,128]{1,0:T(8,128)S(1)}, f32[32,128]{1,0:T(8,128)S(1)}, u32[]{:S(2)}, u32[]{:S(2)}) %collective-permute-start.2) | collective-permute-done | bytes 16416 | tf_op jit(solution)/shard_map/ppermute | solution.py:261
  81.6 15.7 %all_to_all.23 = f32[16,32,128]{2,1,0:T(8,128)S(1)} all-to-all(f32[16,32,128]{2,1,0:T(8,128)S(1)} %broadcast_in_dim.8), channel_id=1, replica_groups=mesh['xl'=2,'y'=8,'core'=2,'xh'=2,'z'=8] {'xh','z'}, dimensions={0} | all-to-all | bytes 524288 | tf_op jit(solution)/shard_map/all_to_all | solution.py:244
  97.4 0.7 reverse_select_fusion
  (8 shorter events, 0.1 us)
Async XLA Ops:
  1.2 4.0 %collective-permute-start = (f32[1280,128]{1,0:T(8,128)S(1)}, f32[1280,128]{1,0:T(8,128)S(1)}, u32[]{:S(2)}, u32[]{:S(2)}) collective-permute-start(f32[1280,128]{1,0:T(8,128)S(1)} %get-tuple-element.14.sent_ref), channel_id=1, source_target_pairs={{0,16},{16,0},{1,17},{17,1},{2,18},{18,2},{3,19},{19,3},{4,20},{20... | collective-permute-start | bytes 1966088 | tf_op jit(solution)/shard_map/ppermute | solution.py:237
  24.9 11.6 %collective-permute-start.1 = (f32[32,128]{1,0:T(8,128)S(1)}, f32[32,128]{1,0:T(8,128)S(1)}, u32[]{:S(2)}, u32[]{:S(2)}) collective-permute-start(f32[32,128]{1,0:T(8,128)S(1)} %reduce_sum.18), channel_id=1, source_target_pairs={{0,4},{1,36},{2,68},{3,100},{4,132},{5,164},{6,196},{7,228},{8,260... | collective-permute-start | bytes 49160 | tf_op jit(solution)/shard_map/ppermute | solution.py:259
  72.6 9.0 %collective-permute-start.2 = (f32[32,128]{1,0:T(8,128)S(1)}, f32[32,128]{1,0:T(8,128)S(1)}, u32[]{:S(2)}, u32[]{:S(2)}) collective-permute-start(f32[32,128]{1,0:T(8,128)S(1)} %reduce_sum.19), channel_id=1, source_target_pairs={{0,20},{1,52},{2,84},{3,116},{4,148},{5,180},{6,212},{7,244},{8,26... | collective-permute-start | bytes 49160 | tf_op jit(solution)/shard_map/ppermute | solution.py:261

commit v6 on v4

--- a/solution.py
+++ b/solution.py
@@ -92,10 +92,10 @@
         (buffer_ref,), block)
 
 
-def load_kernel(fronts, init_ref, green_ref, field_ref,
-                sent_ref, mine_ref, last_ref, flag_ref, sems):
-    core, xl, xh, z = (lax.axis_index(axis) for axis in ("core", "xl", "xh", "z"))
-    half, piece, block = mine_ref.shape[0], last_ref.shape[0], green_ref.shape[0]
+def load_kernel(init_ref, green_ref, field_ref,
+                sent_ref, flag_ref, sems):
+    core, xl = lax.axis_index("core"), lax.axis_index("xl")
+    half, block = init_ref.shape[0] // 2, green_ref.shape[0]
 
     def rows_of(index, count):
         return init_ref.at[pl.ds(pl.multiple_of(index * count, count), count)]
@@ -106,8 +106,6 @@
             (rows_of(1 - core, half), sent_ref.at[pl.ds(0, half)]),
             (green_ref, sent_ref.at[pl.ds(half, block)]),
             (field_ref, sent_ref.at[pl.ds(half + block, block)]),
-            (rows_of(core, half), mine_ref),
-            (rows_of((core + 1 + xh + xl) % 2 * fronts + z, piece), last_ref),
         ))
     ]
     for copy in copies:
@@ -117,7 +115,20 @@
         copy.wait()
 
 
-def near_kernel(orbits, order, block, mine_ref, sent_ref, own_ref):
+def near_kernel(orbits, order, block, init_ref, sent_ref, own_ref, mine_ref, last_ref, sems):
+    core, xl, xh, z = (lax.axis_index(axis) for axis in ("core", "xl", "xh", "z"))
+    half, piece = mine_ref.shape[0], last_ref.shape[0]
+    last = ((core + 1 + xh + xl) % 2 * len(order) + z) * piece
+    copies = [
+        pltpu.make_async_copy(
+            init_ref.at[pl.ds(pl.multiple_of(start, count), count)], target, sems.at[n])
+        for n, (start, count, target) in enumerate(
+            ((core * half, half, mine_ref), (last, piece, last_ref)))
+    ]
+    for copy in copies:
+        copy.start()
+    for copy in copies:
+        copy.wait()
     for part, image in enumerate(half_image(mine_ref, sent_ref, orbits, block)):
         put(own_ref, part, image, orbits, order)
 
@@ -163,35 +174,38 @@
 LIMIT = pltpu.CompilerParams(vmem_limit_bytes=12 << 20)
 
 
-def load(init, green, field, fronts):
+def load(init, green, field):
     rows, width = init.shape
     operands = [pltpu.with_memory_space_constraint(x, pltpu.HBM) for x in (init, green, field)]
     return pl.pallas_call(
-        functools.partial(load_kernel, fronts // 2),
+        load_kernel,
         out_shape=[
             jax.ShapeDtypeStruct((n, width), kind) for n, kind in (
-                (rows // 2 + 2 * green.shape[0], jnp.float32), (rows // 2, jnp.float32),
-                (rows // fronts, jnp.float32), (8, jnp.int32))
+                (rows // 2 + 2 * green.shape[0], jnp.float32), (8, jnp.int32))
         ],
         in_specs=[pl.BlockSpec(memory_space=pltpu.HBM)] * 3,
-        out_specs=[VMEM] * 4,
-        scratch_shapes=[pltpu.SemaphoreType.DMA((5,))],
+        out_specs=[VMEM] * 2,
+        scratch_shapes=[pltpu.SemaphoreType.DMA((3,))],
         compiler_params=LIMIT,
         name="load",
     )(*operands)
 
 
-def near_collide(mine, sent, orbits, order, block):
-    rows, width = mine.shape
+def near_collide(init, sent, orbits, order, block):
+    rows, width = init.shape
+    init = pltpu.with_memory_space_constraint(init, pltpu.HBM)
     return pl.pallas_call(
         functools.partial(near_kernel, orbits, order, block),
-        out_shape=jax.ShapeDtypeStruct((2 * rows, width), jnp.float32),
-        in_specs=[VMEM] * 2,
-        out_specs=VMEM,
+        out_shape=[
+            jax.ShapeDtypeStruct((n, width), jnp.float32) for n in (rows, rows // 2, 2 * orbits)
+        ],
+        in_specs=[pl.BlockSpec(memory_space=pltpu.HBM), VMEM],
+        out_specs=[VMEM] * 3,
+        scratch_shapes=[pltpu.SemaphoreType.DMA((2,))],
         compiler_params=LIMIT,
         cost_estimate=pl.CostEstimate(flops=10**8, bytes_accessed=10**6, transcendentals=0),
         name="near_collide",
-    )(mine, sent)
+    )(init, sent)
 
 
 def far_collide(mine, own, got, orbits, order, block):
@@ -250,9 +264,9 @@
     green, field = tiles(green_hist), tiles(field_hist)
     order = [(y + zs // 2) % zs for y in range(ys)]
     block = green.shape[0]
-    sent, mine, last, flag = load(init, green, field, fronts)
+    sent, flag = load(init, green, field)
     got = swap(sent)
-    own = near_collide(mine, sent, orbits, order, block)
+    own, mine, last = near_collide(init, sent, orbits, order, block)
     flag = jnp.broadcast_to(flag == 0, (2, rows // 16, 8, width))
     own, flag = lax.optimization_barrier((own, flag))
     chip, near = far_collide(mine, own, got, orbits, order, block)

time: 98.4 us -> 98.4 us (level)
  transfers between devices with their start and end apart: 3 -> 3, of which waited for: 3 -> 3; matrix products, arithmetic and copies ran while one was open for 0% -> 0% of each run, Pallas kernels for 1% -> 2%
where the time goes in v6:
time: 98.4 us; the launch traced here: 98.1 us
  blocking collectives  69.6 us (71%)
  starting transfers between devices  14.1 us (14%)
  waiting for transfers between devices  8.84 us (9%)
  Pallas kernels  4.57 us (5%)
    all_to_all x2, blocking collectives, gathered(): return lax.all_to_all(copies, B, 0, 0, tiled=True).reshape(rows, width)  37.1 us
    all_to_all x2, blocking collectives, reduced(): lax.all_to_all(partial_sum.reshape(fronts, -1, width), A, 0, 0, tiled=True)  32.6 us
    ppermute x1, starting transfers between devices, corrector(): lax.ppermute(reduced(chip), EVERY, turns[0])  10.2 us
    ppermute x1, waiting for transfers between devices, corrector(): turned = lax.ppermute(reduced(image), EVERY, turns[1])  7.04 us
  transfers between devices with their start and end apart: 3, of which 3 were waited for; matrix products, arithmetic and copies ran while one was open for 0% of the time, Pallas kernels for 2%

profile of v6, /device:TPU:8, one launch (start us, length us, event | category | flops | bytes accessed | tf_op | source)
XLA Modules:
  0.0 98.1 jit_solution(11389412831028119936)
XLA Ops:
  0.0 1.1 %load.1 = (f32[1280,128]{1,0:T(8,128)S(1)}, s32[8,128]{1,0:T(8,128)S(1)}) custom-call(f32[512,128]{1,0:T(8,128)} %bitcast.19, f32[512,128]{1,0:T(8,128)} %bitcast.22, f32[512,128]{1,0:T(8,128)} %bitcast.23), custom_call_target="tpu_custom_call" | custom-call | tf_op jit(solution)/shard_map/load/pallas_call | solution.py:180
  1.1 1.9 %collective-permute-start = (f32[1280,128]{1,0:T(8,128)S(1)}, f32[1280,128]{1,0:T(8,128)S(1)}, u32[]{:S(2)}, u32[]{:S(2)}) collective-permute-start(f32[1280,128]{1,0:T(8,128)S(1)} %get-tuple-element.14.sent_ref), channel_id=1, source_target_pairs={{0,16},{16,0},{1,17},{17,1},{2,18},{18,2},{3,19},{19,3},{4,20},{20... | collective-permute-start | bytes 1966088 | tf_op jit(solution)/shard_map/ppermute | solution.py:251
  3.1 1.6 %near_collide.1 = (f32[512,128]{1,0:T(8,128)S(1)}, f32[256,128]{1,0:T(8,128)S(1)}, f32[32,128]{1,0:T(8,128)S(1)}) custom-call(f32[512,128]{1,0:T(8,128)} %bitcast.20, f32[1280,128]{1,0:T(8,128)S(1)} %get-tuple-element.14.sent_ref), custom_call_target="tpu_custom_call" | custom-call | flops 100000000 | bytes 1000000 | tf_op jit(solution)/shard_map/near_collide/pallas_call | solution.py:197
  4.7 0.4 collective-permute-done.got_ref
  5.1 0.7 far_collide.1
  5.8 19.0 %all_to_all.20 = f32[16,32,128]{2,1,0:T(8,128)S(1)} all-to-all(f32[16,32,128]{2,1,0:T(8,128)S(1)} %bitcast.18), channel_id=1, replica_groups=mesh['xl'=2,'y'=8,'core'=2,'xh'=2,'z'=8] {'xl','y'}, dimensions={0} | all-to-all | bytes 524288 | tf_op jit(solution)/shard_map/all_to_all | solution.py:254
  24.9 10.2 %collective-permute-start.1 = (f32[32,128]{1,0:T(8,128)S(1)}, f32[32,128]{1,0:T(8,128)S(1)}, u32[]{:S(2)}, u32[]{:S(2)}) collective-permute-start(f32[32,128]{1,0:T(8,128)S(1)} %reduce_sum.18), channel_id=1, source_target_pairs={{0,4},{1,36},{2,68},{3,100},{4,132},{5,164},{6,196},{7,228},{8,260... | collective-permute-start | bytes 49160 | tf_op jit(solution)/shard_map/ppermute | solution.py:273
  35.1 1.4 %collective-permute-done.1 = f32[32,128]{1,0:T(8,128)S(1)} collective-permute-done((f32[32,128]{1,0:T(8,128)S(1)}, f32[32,128]{1,0:T(8,128)S(1)}, u32[]{:S(2)}, u32[]{:S(2)}) %collective-permute-start.1) | collective-permute-done | bytes 16416 | tf_op jit(solution)/shard_map/ppermute | solution.py:273
  36.5 21.3 %all_to_all.21 = f32[16,32,128]{2,1,0:T(8,128)S(1)} all-to-all(f32[16,32,128]{2,1,0:T(8,128)S(1)} %broadcast_in_dim.7), channel_id=1, replica_groups=mesh['xl'=2,'y'=8,'core'=2,'xh'=2,'z'=8] {'xh','z'}, dimensions={0} | all-to-all | bytes 524288 | tf_op jit(solution)/shard_map/all_to_all | solution.py:258
  57.9 1.1 %second_collide.1 = f32[512,128]{1,0:T(8,128)S(1)} custom-call(f32[512,128]{1,0:T(8,128)S(1)} %bitcast.16, f32[1280,128]{1,0:T(8,128)S(1)} %get-tuple-element.14.sent_ref, f32[1280,128]{1,0:T(8,128)S(1)} %collective-permute-done.got_ref), custom_call_target="tpu_custom_call" | custom-call | tf_op jit(solution)/shard_map/second_collide/pallas_call | solution.py:226
  59.0 13.6 %all_to_all.22 = f32[16,32,128]{2,1,0:T(8,128)S(1)} all-to-all(f32[16,32,128]{2,1,0:T(8,128)S(1)} %bitcast.17), channel_id=1, replica_groups=mesh['xl'=2,'y'=8,'core'=2,'xh'=2,'z'=8] {'xl','y'}, dimensions={0} | all-to-all | bytes 524288 | tf_op jit(solution)/shard_map/all_to_all | solution.py:254
  72.6 1.9 %collective-permute-start.2 = (f32[32,128]{1,0:T(8,128)S(1)}, f32[32,128]{1,0:T(8,128)S(1)}, u32[]{:S(2)}, u32[]{:S(2)}) collective-permute-start(f32[32,128]{1,0:T(8,128)S(1)} %reduce_sum.19), channel_id=1, source_target_pairs={{0,20},{1,52},{2,84},{3,116},{4,148},{5,180},{6,212},{7,244},{8,26... | collective-permute-start | bytes 49160 | tf_op jit(solution)/shard_map/ppermute | solution.py:275
  74.5 7.0 %collective-permute-done.2 = f32[32,128]{1,0:T(8,128)S(1)} collective-permute-done((f32[32,128]{1,0:T(8,128)S(1)}, f32[32,128]{1,0:T(8,128)S(1)}, u32[]{:S(2)}, u32[]{:S(2)}) %collective-permute-start.2) | collective-permute-done | bytes 16416 | tf_op jit(solution)/shard_map/ppermute | solution.py:275
  81.6 15.7 %all_to_all.23 = f32[16,32,128]{2,1,0:T(8,128)S(1)} all-to-all(f32[16,32,128]{2,1,0:T(8,128)S(1)} %broadcast_in_dim.8), channel_id=1, replica_groups=mesh['xl'=2,'y'=8,'core'=2,'xh'=2,'z'=8] {'xh','z'}, dimensions={0} | all-to-all | bytes 524288 | tf_op jit(solution)/shard_map/all_to_all | solution.py:258
  97.3 0.7 reverse_select_fusion
  (8 shorter events, 0.1 us)
Async XLA Ops:
  1.1 4.0 %collective-permute-start = (f32[1280,128]{1,0:T(8,128)S(1)}, f32[1280,128]{1,0:T(8,128)S(1)}, u32[]{:S(2)}, u32[]{:S(2)}) collective-permute-start(f32[1280,128]{1,0:T(8,128)S(1)} %get-tuple-element.14.sent_ref), channel_id=1, source_target_pairs={{0,16},{16,0},{1,17},{17,1},{2,18},{18,2},{3,19},{19,3},{4,20},{20... | collective-permute-start | bytes 1966088 | tf_op jit(solution)/shard_map/ppermute | solution.py:251
  24.9 11.6 %collective-permute-start.1 = (f32[32,128]{1,0:T(8,128)S(1)}, f32[32,128]{1,0:T(8,128)S(1)}, u32[]{:S(2)}, u32[]{:S(2)}) collective-permute-start(f32[32,128]{1,0:T(8,128)S(1)} %reduce_sum.18), channel_id=1, source_target_pairs={{0,4},{1,36},{2,68},{3,100},{4,132},{5,164},{6,196},{7,228},{8,260... | collective-permute-start | bytes 49160 | tf_op jit(solution)/shard_map/ppermute | solution.py:273
  72.6 9.0 %collective-permute-start.2 = (f32[32,128]{1,0:T(8,128)S(1)}, f32[32,128]{1,0:T(8,128)S(1)}, u32[]{:S(2)}, u32[]{:S(2)}) collective-permute-start(f32[32,128]{1,0:T(8,128)S(1)} %reduce_sum.19), channel_id=1, source_target_pairs={{0,20},{1,52},{2,84},{3,116},{4,148},{5,180},{6,212},{7,244},{8,26... | collective-permute-start | bytes 49160 | tf_op jit(solution)/shard_map/ppermute | solution.py:275
